TPU v7x, 128 devices: a whole 4x4x4 slice. The times are simulated.
128 devices in a mesh: seq: 32 (over z, x, y_hi), head: 4 (over y_lo, core).
Axes of the slice: x: 4, y: 4 (y_hi: 2, y_lo: 2; y = y_hi * 2 + y_lo), z: 4, core: 2. Of those that a mesh axis runs over, the one named last changes fastest.
Arguments:
- tokens: bfloat16 [8192, 2048], P('seq'), may hold values from -6 to 6
- input_gain: float32 [2048], replicated, may hold values from 0.1 to 1.9
- w_query: bfloat16 [2048, 4096], P(None, 'head'), may hold values from -0.125 to 0.125
- w_key: bfloat16 [2048, 512], P(None, 'head'), may hold values from -0.125 to 0.125
- w_value: bfloat16 [2048, 512], P(None, 'head'), may hold values from -0.125 to 0.125
- query_gain: float32 [128], replicated, may hold values from 1 to 8
- key_gain: float32 [128], replicated, may hold values from 1 to 8
- w_out: bfloat16 [4096, 2048], P('head'), may hold values from -0.09375 to 0.09375
- post_gain: float32 [2048], replicated, may hold values from 0.1 to 1.9
- expert_ids: int32 [8192, 8], P(('seq', 'head')), may hold values from 0 to 127, all different within a row; in each aligned block of 64 rows (0 to 63, 64 to 127, ...) at most 6 rows name the same one
- route_weights: float32 [8192, 8], P(('seq', 'head')), may hold values from 0.05 to 1
- w_gate: bfloat16 [128, 2048, 768], P(('seq', 'head')), may hold values from -0.125 to 0.125
- w_up: bfloat16 [128, 2048, 768], P(('seq', 'head')), may hold values from -0.125 to 0.125
- w_down: bfloat16 [128, 768, 2048], P(('seq', 'head')), may hold values from -0.21875 to 0.21875
Outputs:
- layer_out: bfloat16 [8192, 2048], P(('seq', 'head'))
Inputs may be any that keep to these rules, and one draw needn't show every extreme that they name: `expert_ids`: the 8 experts of a token differ. In the rows of one device (64 tokens, aligned blocks), no expert is named more than 6 times.
All inputs are finite; a program needn't handle non-finite values.
Results may differ from a plain program's by a relative error of at most 0.012.
The roundings to bfloat16 on the way count: a program that leaves them out, or rounds other values in their place, can miss the bound.
Values may be sent and summed in bfloat16 or wider, within the bound.
A program may use at most 128 MiB of HBM per device.

v0:
```python
import functools

import jax
import jax.numpy as jnp
from jax import lax
from jax.experimental import pallas as pl
from jax.experimental.pallas import tpu as pltpu
from jax.sharding import PartitionSpec as P

MESH = pl.DeviceIdType.MESH
EPSILON = 1e-06
THETA = 1000000.0
LOG2E = 1.4426950408889634
GROUP = 4
CAPACITY = 6


def attention_kernel(
    seq_count, heads, rows, dim, kv_ref, q_ref, out_ref, kvbuf, m_s, l_s, acc, send_sem, recv_sem, own_sem
):
    i = lax.axis_index("seq")
    h = lax.axis_index("head")
    barrier = pltpu.get_barrier_semaphore()

    def greet(j, c):
        @pl.when(j != i)
        def _():
            pl.semaphore_signal(barrier, inc=1, device_id=(j, h), device_id_type=MESH)

        return c

    lax.fori_loop(0, seq_count, greet, 0)
    own = pltpu.make_async_copy(kv_ref, kvbuf.at[i], own_sem)
    own.start()
    first_group = i // GROUP
    for u in range(GROUP):

        @pl.when(first_group * GROUP + u > i)
        def _():
            kvbuf[first_group * GROUP + u] = jnp.zeros(kvbuf.shape[1:], kvbuf.dtype)

    pl.semaphore_wait(barrier, seq_count - 1)

    def push(peer):
        return pltpu.make_async_remote_copy(
            src_ref=kv_ref,
            dst_ref=kvbuf.at[i],
            send_sem=send_sem.at[peer],
            recv_sem=recv_sem.at[i],
            device_id=(peer, h),
            device_id_type=MESH,
        )

    def arrival(source):
        return pltpu.make_async_remote_copy(
            src_ref=kv_ref,
            dst_ref=kvbuf.at[source],
            send_sem=send_sem.at[source],
            recv_sem=recv_sem.at[source],
            device_id=(source, h),
            device_id_type=MESH,
        )

    def start(t, c):
        peer = lax.rem(i + t * 13, seq_count)

        @pl.when(peer > i)
        def _():
            push(peer).start()

        return c

    lax.fori_loop(1, seq_count, start, 0)
    own.wait()
    scale = dim ** (-0.5) * LOG2E

    def group(g, masked):
        for u in range(GROUP):

            @pl.when(g * GROUP + u < i)
            def _():
                arrival(g * GROUP + u).wait_recv()

        keys = jnp.concatenate([kvbuf[g * GROUP + u, 0:rows, :] for u in range(GROUP)], axis=0)
        halves = [
            kvbuf[g * GROUP + u, rows + dim * w : rows + dim * (w + 1), :]
            for u in range(GROUP)
            for w in range(rows // dim)
        ]
        values = jnp.concatenate(halves, axis=1)
        values = jnp.concatenate([values, jnp.ones((16, values.shape[1]), values.dtype)], axis=0)
        scores = jnp.dot(keys, q_ref[...], preferred_element_type=jnp.float32)
        if masked:
            key_at = lax.broadcasted_iota(jnp.int32, scores.shape, 0)
            query_at = lax.broadcasted_iota(jnp.int32, scores.shape, 1) % rows + (i - g * GROUP) * rows
            scores = jnp.where(key_at <= query_at, scores, -1e30)
        top = jnp.max(scores, axis=0, keepdims=True)
        if not masked:
            top = jnp.maximum(top, m_s[...])
        weights = jnp.exp2(scores * scale - top * scale)
        mixed = jnp.dot(values, weights.astype(jnp.bfloat16), preferred_element_type=jnp.float32)
        if masked:
            l_s[...] = mixed[dim : dim + 1]
            acc[...] = mixed[:dim]
        else:
            shrink = jnp.exp2((m_s[...] - top) * scale)
            l_s[...] = l_s[...] * shrink + mixed[dim : dim + 1]
            acc[...] = acc[...] * shrink + mixed[:dim]
        m_s[...] = top

    group(first_group, True)

    def earlier(t, c):
        group(first_group - t, False)
        return c

    lax.fori_loop(1, first_group + 1, earlier, 0)
    for head in range(heads):
        columns = slice(head * rows, (head + 1) * rows)
        part = acc[:, columns] / l_s[:, columns]
        out_ref[:, head * dim : (head + 1) * dim] = part.T.astype(jnp.bfloat16)

    def finish(peer, c):
        @pl.when(peer > i)
        def _():
            push(peer).wait_send()

        return c

    lax.fori_loop(0, seq_count, finish, 0)


def attention(kv, q, seq_count, heads, rows, dim):
    return pl.pallas_call(
        functools.partial(attention_kernel, seq_count, heads, rows, dim),
        out_shape=jax.ShapeDtypeStruct((rows, heads * dim), jnp.bfloat16),
        in_specs=[pl.BlockSpec(memory_space=pltpu.VMEM)] * 2,
        out_specs=pl.BlockSpec(memory_space=pltpu.VMEM),
        scratch_shapes=[
            pltpu.VMEM((seq_count,) + kv.shape, jnp.bfloat16),
            pltpu.VMEM((1, heads * rows), jnp.float32),
            pltpu.VMEM((1, heads * rows), jnp.float32),
            pltpu.VMEM((dim, heads * rows), jnp.float32),
            pltpu.SemaphoreType.DMA((seq_count,)),
            pltpu.SemaphoreType.DMA((seq_count,)),
            pltpu.SemaphoreType.DMA,
        ],
        compiler_params=pltpu.CompilerParams(
            collective_id=0, has_side_effects=True, vmem_limit_bytes=50 << 20
        ),
        name="attention",
    )(kv, q)


def cut_along(array, dim, devices):
    dims = array.shape
    blocks = array.reshape(*dims[:dim], devices, dims[dim] // devices, *dims[dim + 1 :])
    return jnp.moveaxis(blocks, dim, 0)


def rms_scale(vectors, gain_vector):
    mean_sq = jnp.mean(vectors * vectors, axis=-1, keepdims=True)
    return vectors * lax.rsqrt(mean_sq + EPSILON) * gain_vector


def rotate(vectors, positions):
    half_dim = vectors.shape[-1] // 2
    frequency = THETA ** (-jnp.arange(half_dim, dtype=jnp.float32) * 2.0 / vectors.shape[-1])
    angles = positions[:, None] * frequency[None, :]
    cosine_table = jnp.cos(angles)[:, None, :]
    sine_table = jnp.sin(angles)[:, None, :]
    front_half = vectors[..., :half_dim]
    back_half = vectors[..., half_dim:]
    return jnp.concatenate(
        [
            front_half * cosine_table - back_half * sine_table,
            back_half * cosine_table + front_half * sine_table,
        ],
        axis=-1,
    )


def neighbour(s, h, step, sign):
    z, x, y, core = s // 8, lax.rem(s // 2, 4), lax.rem(s, 2) * 2 + h // 2, lax.rem(h, 2)
    turn = lax.rem(step * 37, 128)
    z = lax.rem(z + sign * (turn // 32) + 4, 4)
    x = lax.rem(x + sign * lax.rem(turn // 8, 4) + 4, 4)
    y = lax.rem(y + sign * lax.rem(turn // 2, 4) + 4, 4)
    core = lax.rem(core + lax.rem(turn, 2), 2)
    return z * 8 + x * 2 + y // 2, lax.rem(y, 2) * 2 + core


def expert_kernel(
    cap,
    chunks,
    idx_ref,
    slot_ref,
    mix_ref,
    own_ref,
    part_ref,
    gain_ref,
    gate_hbm,
    up_hbm,
    down_hbm,
    out_ref,
    gate,
    up,
    down,
    wide,
    home,
    tiles,
    outgoing,
    arrived,
    batch,
    results,
    returned,
    weight_sem,
    send_out,
    recv_out,
    send_back,
    recv_back,
):
    s = lax.axis_index("seq")
    h = lax.axis_index("head")
    me = s * 4 + h
    count = 128
    rows, width = own_ref.shape
    cuts = width // 128
    barrier = pltpu.get_barrier_semaphore()

    def greet(t, c):
        pl.semaphore_signal(barrier, inc=1, device_id=neighbour(s, h, t, 1), device_id_type=MESH)
        return c

    lax.fori_loop(1, count, greet, 0)
    loads = [
        pltpu.make_async_copy(hbm, vmem, weight_sem.at[n])
        for n, (hbm, vmem) in enumerate(((gate_hbm, gate), (up_hbm, up), (down_hbm, down)))
    ]
    for load in loads:
        load.start()
    residual = own_ref[...].astype(jnp.float32)
    for n in range(part_ref.shape[0]):
        residual = residual + part_ref[n].astype(jnp.float32)
    mean_sq = jnp.mean(residual * residual, axis=-1, keepdims=True)
    routed = residual * lax.rsqrt(mean_sq + EPSILON) * gain_ref[...]
    span = rows * cuts
    for c in range(cuts):
        columns = slice(c * 128, (c + 1) * 128)
        home[pl.ds(c, rows, stride=cuts), :] = residual[:, columns]
        wide[pl.ds(c, rows, stride=cuts), :] = routed[:, columns]
    tiles[...] = wide[0:span, :].astype(jnp.bfloat16).reshape(tiles.shape)
    pl.semaphore_wait(barrier, count - 1)

    def fill(t, target, ref, at):
        for c in range(cap):
            token = idx_ref[target * cap + c]
            ref[at * cap + c] = tiles[token]

    def part(ref, t):
        return ref.at[pl.ds(t * cap, cap)]

    def dispatch(t):
        return pltpu.make_async_remote_copy(
            src_ref=part(outgoing, t),
            dst_ref=part(arrived, t),
            send_sem=send_out.at[t],
            recv_sem=recv_out.at[t],
            device_id=neighbour(s, h, t, 1),
            device_id_type=MESH,
        )

    def give_back(t):
        return pltpu.make_async_remote_copy(
            src_ref=part(results, t),
            dst_ref=part(returned, me),
            send_sem=send_back.at[t],
            recv_sem=recv_back.at[me],
            device_id=neighbour(s, h, t, -1),
            device_id_type=MESH,
        )

    def come_back(t):
        ts, th = neighbour(s, h, t, 1)
        expert = ts * 4 + th
        return pltpu.make_async_remote_copy(
            src_ref=part(results, t),
            dst_ref=part(returned, expert),
            send_sem=send_back.at[t],
            recv_sem=recv_back.at[expert],
            device_id=(ts, th),
            device_id_type=MESH,
        )

    def post(t, c):
        ts, th = neighbour(s, h, t, 1)
        fill(t, ts * 4 + th, outgoing, t)
        dispatch(t).start()
        return c

    lax.fori_loop(1, count, post, 0)
    fill(0, me, arrived, 0)
    for load in loads:
        load.wait()
    each = count // chunks
    size = each * cap

    def work(k, c):
        def await_one(t, c):
            @pl.when(t > 0)
            def _():
                dispatch(t).wait_recv()

            return c

        lax.fori_loop(k * each, (k + 1) * each, await_one, 0)
        place = pl.ds(k * size, size)
        wide[...] = arrived[place].astype(jnp.float32).reshape(wide.shape)
        for c in range(cuts):
            batch[:, c * 128 : (c + 1) * 128] = wide[pl.ds(c, size, stride=cuts), :].astype(jnp.bfloat16)
        gate_proj = jnp.dot(batch[...], gate[...], preferred_element_type=jnp.float32)
        up_proj = jnp.dot(batch[...], up[...], preferred_element_type=jnp.float32)
        hidden = (gate_proj / (1.0 + jnp.exp(-gate_proj)) * up_proj).astype(jnp.bfloat16)
        result = jnp.dot(hidden, down[...], preferred_element_type=jnp.float32)
        for c in range(cuts):
            wide[pl.ds(c, size, stride=cuts), :] = result[:, c * 128 : (c + 1) * 128]
        results[place] = wide[...].astype(jnp.bfloat16).reshape(size, cuts, 128)

        def answer(t, c):
            @pl.when(t > 0)
            def _():
                give_back(t).start()

            return c

        lax.fori_loop(k * each, (k + 1) * each, answer, 0)
        return c

    lax.fori_loop(0, chunks, work, 0)
    returned[pl.ds(me * cap, cap)] = results[0:cap]

    def settle(t, c):
        come_back(t).wait_recv()
        return c

    lax.fori_loop(1, count, settle, 0)
    top = mix_ref.shape[0] // rows

    def combine(t, c):
        place = pl.ds(pl.multiple_of(t * cuts, cuts), cuts)
        total = jnp.zeros((cuts, 128), jnp.float32)
        for k in range(top):
            row = returned[slot_ref[t * top + k]]
            total = total + row.astype(jnp.float32) * mix_ref[t * top + k]
        home[place, :] = home[place, :] + total
        return c

    lax.fori_loop(0, rows, combine, 0)
    for c in range(cuts):
        out_ref[:, c * 128 : (c + 1) * 128] = home[pl.ds(c, rows, stride=cuts), :].astype(jnp.bfloat16)

    def finish(t, c):
        dispatch(t).wait_send()
        give_back(t).wait_send()
        return c

    lax.fori_loop(1, count, finish, 0)


def experts(idx, slot, mix, own, parts, gain, w_gate, w_up, w_down, cap):
    rows, width = own.shape
    depth, hidden = w_gate.shape
    cuts = width // 128
    count = 128
    chunks = 4
    size = count * cap // chunks
    smem = pl.BlockSpec(memory_space=pltpu.SMEM)
    vmem = pl.BlockSpec(memory_space=pltpu.VMEM)
    hbm = pl.BlockSpec(memory_space=pl.ANY)
    tiled = pltpu.VMEM((count * cap, cuts, 128), jnp.bfloat16)
    return pl.pallas_call(
        functools.partial(expert_kernel, cap, chunks),
        out_shape=jax.ShapeDtypeStruct((rows, width), jnp.bfloat16),
        in_specs=[smem, smem, smem, vmem, vmem, vmem, hbm, hbm, hbm],
        out_specs=vmem,
        scratch_shapes=[
            pltpu.VMEM((depth, hidden), jnp.bfloat16),
            pltpu.VMEM((depth, hidden), jnp.bfloat16),
            pltpu.VMEM((hidden, depth), jnp.bfloat16),
            pltpu.VMEM((size * cuts, 128), jnp.float32),
            pltpu.VMEM((rows * cuts, 128), jnp.float32),
            pltpu.VMEM((rows, cuts, 128), jnp.bfloat16),
            tiled,
            tiled,
            pltpu.VMEM((size, width), jnp.bfloat16),
            tiled,
            tiled,
            pltpu.SemaphoreType.DMA((3,)),
            pltpu.SemaphoreType.DMA((count,)),
            pltpu.SemaphoreType.DMA((count,)),
            pltpu.SemaphoreType.DMA((count,)),
            pltpu.SemaphoreType.DMA((count,)),
        ],
        compiler_params=pltpu.CompilerParams(
            collective_id=1, has_side_effects=True, vmem_limit_bytes=50 << 20
        ),
        name="experts",
    )(idx, slot, mix, own, parts, gain, w_gate, w_up, w_down)


def body(
    tokens,
    input_gain,
    w_query,
    w_key,
    w_value,
    query_gain,
    key_gain,
    w_out,
    post_gain,
    expert_ids,
    route_weights,
    w_gate,
    w_up,
    w_down,
):
    tok_rows, width = tokens.shape
    head_dim = query_gain.shape[0]
    heads_here = w_query.shape[1] // head_dim
    seq_count = lax.axis_size("seq")
    seq_index = lax.axis_index("seq")
    head_count = lax.axis_size("head")
    head_index = lax.axis_index("head")
    normed = rms_scale(tokens.astype(jnp.float32), input_gain).astype(jnp.bfloat16)
    offset = seq_index * tok_rows
    positions = (offset + jnp.arange(tok_rows, dtype=jnp.int32)).astype(jnp.float32)
    queries = jnp.dot(normed, w_query, preferred_element_type=jnp.float32).reshape(
        tok_rows, heads_here, head_dim
    )
    queries = rotate(rms_scale(queries, query_gain), positions).astype(jnp.bfloat16)
    key_rows = jnp.dot(normed, w_key, preferred_element_type=jnp.float32).reshape(
        tok_rows, 1, head_dim
    )
    key_rows = (
        rotate(rms_scale(key_rows, key_gain), positions)
        .astype(jnp.bfloat16)
        .reshape(tok_rows, head_dim)
    )
    value_rows = jnp.dot(normed, w_value, preferred_element_type=jnp.float32).astype(jnp.bfloat16)
    queries = queries.transpose(2, 1, 0).reshape(head_dim, heads_here * tok_rows)
    value_t = value_rows.T.reshape(head_dim, tok_rows // head_dim, head_dim)
    value_t = value_t.transpose(1, 0, 2).reshape(tok_rows, head_dim)
    kv_block = jnp.concatenate([key_rows, value_t], axis=0)
    attended = attention(kv_block, queries, seq_count, heads_here, tok_rows, head_dim)
    rows_here = tok_rows // head_count
    own_rows = lax.dynamic_slice_in_dim(tokens, head_index * rows_here, rows_here, 0)
    products = jnp.dot(attended, w_out, preferred_element_type=jnp.float32).astype(jnp.bfloat16)
    parts = lax.all_to_all(
        cut_along(products, 0, head_count), "head", split_axis=0, concat_axis=0, tiled=True
    )
    experts_all = w_gate.shape[0] * seq_count * head_count
    top_count = expert_ids.shape[1]
    onehot = expert_ids[:, :, None] == jnp.arange(experts_all, dtype=jnp.int32)
    named = jnp.any(onehot, axis=1)
    earlier = (jnp.arange(rows_here)[:, None] > jnp.arange(rows_here)[None, :]).astype(jnp.bfloat16)
    rank = jnp.dot(earlier, named.astype(jnp.bfloat16), preferred_element_type=jnp.float32)
    rank = rank.astype(jnp.int32)
    slot = expert_ids * CAPACITY + jnp.sum(jnp.where(onehot, rank[:, None, :], 0), axis=2)
    chosen = named[:, :, None] & (rank[:, :, None] == jnp.arange(CAPACITY, dtype=jnp.int32))
    idx = jnp.sum(jnp.where(chosen, jnp.arange(rows_here, dtype=jnp.int32)[:, None, None], 0), axis=0)
    mixing = route_weights / jnp.sum(route_weights, axis=1, keepdims=True)
    return experts(
        idx.reshape(-1),
        slot.reshape(-1),
        mixing.reshape(-1),
        own_rows,
        parts,
        post_gain.reshape(1, -1),
        w_gate[0],
        w_up[0],
        w_down[0],
        CAPACITY,
    )


def solution(mesh):
    placed = (
        P("seq", None),
        P(),
        P(None, "head"),
        P(None, "head"),
        P(None, "head"),
        P(),
        P(),
        P("head", None),
        P(),
        P(("seq", "head"), None),
        P(("seq", "head"), None),
        P(("seq", "head"), None, None),
        P(("seq", "head"), None, None),
        P(("seq", "head"), None, None),
    )
    return jax.shard_map(
        body, mesh=mesh, in_specs=placed, out_specs=P(("seq", "head"), None), check_vma=False
    )
```

profile of v0, /device:TPU:2, one launch (start us, length us, event | category | flops | bytes accessed | tf_op | source)
XLA Modules:
  0.0 210.4 jit_solution(5222710808361052516)
XLA Ops:
  0.0 1.6 fusion
  1.6 3.8 %convolution_bitcast_fusion = f32[32,8,8,128]{3,1,2,0:T(8,128)S(1)} fusion(bf16[2048,1024]{1,0:T(8,128)(2,1)} %param.16, bf16[256,2048]{1,0:T(8,128)(2,1)} %param.14, f32[2048]{0:T(1024)} %param.15, f32[256]{0:T(256)S(1)} %add_rsqrt_fusion.2), kind=kOutput, calls=%fused_computation.6 | convolution fusion | flops 1075838976 | bytes 6300672 | tf_op jit(solution)/shard_map/dot_general | solution.py:437
  5.4 0.2 copy.49
  5.6 0.3 multiply_reduce_fusion
  6.1 0.1 copy.47
  6.2 0.3 multiply_multiply_fusion
  6.6 0.5 multiply_cosine_fusion
  7.1 0.5 subtract_convert_fusion
  7.6 0.3 maximum_bitcast_fusion
  7.9 0.6 copy.48
  8.5 0.1 copy.50
  8.7 0.2 copy-done.2
  8.8 0.6 multiply_reduce_fusion.1
  9.4 0.1 copy.44
  9.5 0.1 multiply_bitcast_fusion
  9.6 0.6 fusion.14
  10.2 0.5 convolution_convert_fusion.1
  10.7 0.1 copy.45
  10.9 0.1 pad_maximum_fusion.kv_ref
  11.0 58.8 %attention.1 = bf16[256,1024]{1,0:T(8,128)(2,1)S(1)} custom-call(bf16[512,128]{1,0:T(8,128)(2,1)S(1)} %pad_maximum_fusion.kv_ref, bf16[128,2048]{1,0:T(8,128)(2,1)S(1)} %bitcast.31), custom_call_target="tpu_custom_call" | custom-call | tf_op jit(solution)/shard_map/attention/pallas_call | solution.py:134
  69.8 4.4 %convolution_convert_fusion = bf16[256,2048]{1,0:T(8,128)(2,1)} fusion(bf16[256,1024]{1,0:T(8,128)(2,1)S(1)} %attention.1, bf16[1024,2048]{1,0:T(8,128)(2,1)} %param.21), kind=kOutput, calls=%fused_computation.2 | convolution fusion | flops 1074266112 | bytes 5767168 | tf_op jit(solution)/shard_map/dot_general | solution.py:457
  74.2 7.0 %all-to-all-start = ((bf16[4,64,2048]{2,1,0:T(8,128)(2,1)}), bf16[4,64,2048]{2,1,0:T(8,128)(2,1)S(1)}, u32[]{:S(2)}, u32[]{:S(2)}) async-start(bf16[4,64,2048]{2,1,0:T(8,128)(2,1)} %bitcast.38), calls=%async_computation | async-start | bytes 2097152 | tf_op jit(solution)/shard_map/all_to_all | solution.py:458
  81.3 0.2 fusion.3
  81.4 0.1 convolution_convert_fusion.2
  81.6 0.1 copy.40
  81.8 0.1 reshape.188.idx_ref
  81.9 1.2 select_reduce_fusion
  83.3 0.1 reshape.189.slot_ref
  83.5 0.1 reshape.190.mix_ref
  83.6 12.0 %all-to-all-done.part_ref = bf16[4,64,2048]{2,1,0:T(8,128)(2,1)S(1)} async-done(((bf16[4,64,2048]{2,1,0:T(8,128)(2,1)}), bf16[4,64,2048]{2,1,0:T(8,128)(2,1)S(1)}, u32[]{:S(2)}, u32[]{:S(2)}) %all-to-all-start) | async-done | bytes 1048608 | tf_op jit(solution)/shard_map/all_to_all | solution.py:458
  95.7 114.0 %experts.1 = bf16[64,2048]{1,0:T(8,128)(2,1)S(1)} custom-call(s32[768]{0:T(1024)S(1)} %reshape.188.idx_ref, s32[512]{0:T(512)S(1)} %reshape.189.slot_ref, f32[512]{0:T(512)S(1)} %reshape.190.mix_ref, bf16[64,2048]{1,0:T(8,128)(2,1)S(1)} %constant_dynamic-slice_fusion.own_ref, bf16[4,64,2048]{2,1,0:T(8,128)(2,1)S(1)} %all-to-all-done.part_ref, ...), custom_call_target="tpu_custom_call" | custom-call | tf_op jit(solution)/shard_map/experts/pallas_call | solution.py:381
  209.7 0.7 copy.52
  (32 shorter events, 0.6 us)
Async XLA Ops:
  0.0 8.6 %copy-start = (bf16[2048,128]{1,0:T(8,128)(2,1)S(1)}, bf16[2048,128]{1,0:T(8,128)(2,1)}, u32[]{:S(2)}) copy-start(bf16[2048,128]{1,0:T(8,128)(2,1)} %param.17) | copy-start | bytes 1572868
  5.4 0.8 copy-start.5
  7.6 1.2 copy-start.2
  7.6 1.2 copy-start.8
  7.9 1.6 copy-start.6
  8.5 1.7 copy-start.7
  74.2 7.0 %copy-start.3 = (s32[64,8]{0,1:T(8,128)S(1)}, s32[64,8]{0,1:T(8,128)}, u32[]{:S(2)}) copy-start(s32[64,8]{0,1:T(8,128)} %param.23) | copy-start | bytes 6148
  74.2 9.2 %copy-start.4 = (f32[64,8]{0,1:T(8,128)S(1)}, f32[64,8]{0,1:T(8,128)}, u32[]{:S(2)}) copy-start(f32[64,8]{0,1:T(8,128)} %param.24) | copy-start | bytes 6148
  74.2 21.5 %copy-start.1 = (f32[2048]{0:T(1024)S(1)}, f32[2048]{0:T(1024)}, u32[]{:S(2)}) copy-start(f32[2048]{0:T(1024)} %param.22) | copy-start | bytes 24580
  74.2 21.5 %all-to-all-start = ((bf16[4,64,2048]{2,1,0:T(8,128)(2,1)}), bf16[4,64,2048]{2,1,0:T(8,128)(2,1)S(1)}, u32[]{:S(2)}, u32[]{:S(2)}) async-start(bf16[4,64,2048]{2,1,0:T(8,128)(2,1)} %bitcast.38), calls=%async_computation | async-start | bytes 2097152 | tf_op jit(solution)/shard_map/all_to_all | solution.py:458
where the time goes:
time: 211 us; the launch traced here: 210 us
  Pallas kernels  173 us (82%)
  waiting for transfers between devices  12 us (6%)
  matrix products  9.46 us (4%)
  starting transfers between devices  6.99 us (3%)
  other arithmetic  5.86 us (3%)
  local copies, waits for them, and re-layouts  2.99 us (1%)
    pallas_call x1, Pallas kernels, experts(): pl.pallas_call(functools.partial(expert_kernel, cap, chunks), out_shape=j...  114 us
    pallas_call x1, Pallas kernels, attention(): pl.pallas_call(functools.partial(attention_kernel, seq_count, heads, rows...  58.8 us
    all_to_all x1, waiting for transfers between devices, body(): lax.all_to_all(cut_along(products, 0, head_count), 'head', split_axis=0,...  12 us
    all_to_all x1, starting transfers between devices, body(): lax.all_to_all(cut_along(products, 0, head_count), 'head', split_axis=0,...  6.99 us
    dot_general x1, matrix products, body(): jnp.dot(attended, w_out, preferred_element_type=jnp.float32)  4.43 us
  transfers between devices with their start and end apart: 1, of which 1 were waited for; matrix products, arithmetic and copies ran while one was open for 1% of the time, Pallas kernels for 0%

commit v1 on v0

--- a/solution.py
+++ b/solution.py
@@ -16,74 +16,110 @@
 
 
 def attention_kernel(
-    seq_count, heads, rows, dim, kv_ref, q_ref, out_ref, kvbuf, m_s, l_s, acc, send_sem, recv_sem, own_sem
+    heads, rows, dim, k_ref, v_ref, q_ref, out_ref, kbuf, vbuf, m_s, l_s, acc, send_k, send_v, recv_k, recv_v
 ):
     i = lax.axis_index("seq")
     h = lax.axis_index("head")
+    count = lax.axis_size("seq")
+    plane = count // 4
+    z, p = i // plane, lax.rem(i, plane)
+    last = i // GROUP
+    for u in range(GROUP):
+
+        @pl.when(last * GROUP + u > i)
+        def _():
+            kbuf[last * GROUP + u] = jnp.zeros(kbuf.shape[1:], kbuf.dtype)
+            vbuf[last * GROUP + u] = jnp.zeros(vbuf.shape[1:], vbuf.dtype)
+
+    kbuf[i] = k_ref[...]
+    vbuf[i] = v_ref[...]
     barrier = pltpu.get_barrier_semaphore()
 
-    def greet(j, c):
-        @pl.when(j != i)
-        def _():
-            pl.semaphore_signal(barrier, inc=1, device_id=(j, h), device_id_type=MESH)
-
-        return c
-
-    lax.fori_loop(0, seq_count, greet, 0)
-    own = pltpu.make_async_copy(kv_ref, kvbuf.at[i], own_sem)
-    own.start()
-    first_group = i // GROUP
-    for u in range(GROUP):
-
-        @pl.when(first_group * GROUP + u > i)
-        def _():
-            kvbuf[first_group * GROUP + u] = jnp.zeros(kvbuf.shape[1:], kvbuf.dtype)
-
-    pl.semaphore_wait(barrier, seq_count - 1)
-
-    def push(peer):
+    def greet(t, c):
+        pl.semaphore_signal(
+            barrier, inc=1, device_id=(lax.rem(i + t, count), h), device_id_type=MESH
+        )
+        return c
+
+    lax.fori_loop(1, count, greet, 0)
+    pl.semaphore_wait(barrier, count - 1)
+
+    def copy(buf, send, recv, at, source, zt, pt):
         return pltpu.make_async_remote_copy(
-            src_ref=kv_ref,
-            dst_ref=kvbuf.at[i],
-            send_sem=send_sem.at[peer],
-            recv_sem=recv_sem.at[i],
-            device_id=(peer, h),
+            src_ref=buf.at[source],
+            dst_ref=buf.at[source],
+            send_sem=send.at[at],
+            recv_sem=recv.at[source],
+            device_id=(zt * plane + pt, h),
             device_id_type=MESH,
         )
 
-    def arrival(source):
-        return pltpu.make_async_remote_copy(
-            src_ref=kv_ref,
-            dst_ref=kvbuf.at[source],
-            send_sem=send_sem.at[source],
-            recv_sem=recv_sem.at[source],
-            device_id=(source, h),
-            device_id_type=MESH,
-        )
-
-    def start(t, c):
-        peer = lax.rem(i + t * 13, seq_count)
-
-        @pl.when(peer > i)
+    def k_column(zt):
+        return copy(kbuf, send_k, recv_k, count + zt, i, zt, p)
+
+    def k_plane(source, pt):
+        return copy(kbuf, send_k, recv_k, source // plane * plane + pt, source, z, pt)
+
+    def v_plane(pt):
+        return copy(vbuf, send_v, recv_v, count + pt, i, z, pt)
+
+    def v_column(source, zt):
+        return copy(vbuf, send_v, recv_v, lax.rem(source, plane) * 4 + zt, source, zt, p)
+
+    def peer(t):
+        return lax.rem(p + t, plane)
+
+    def columns(act):
+        def one(zt, c):
+            act(zt)
+            return c
+
+        lax.fori_loop(z + 1, 4, one, 0)
+
+    def peers(act):
+        def one(t, c):
+            act(peer(t))
+            return c
+
+        lax.fori_loop(1, plane, one, 0)
+
+    def when(cond, act):
+        @pl.when(cond)
         def _():
-            push(peer).start()
-
-        return c
-
-    lax.fori_loop(1, seq_count, start, 0)
-    own.wait()
+            act()
+
+    columns(lambda zt: k_column(zt).start())
+    peers(lambda pt: when((z < 3) | (pt > p), lambda: v_plane(pt).start()))
+    peers(lambda pt: when(pt > p, lambda: k_plane(i, pt).start()))
+    columns(lambda zt: v_column(i, zt).start())
+
+    def pass_k(t, c):
+        source = (z - t) * plane + p
+        k_plane(source, p).wait_recv()
+        peers(lambda pt: k_plane(source, pt).start())
+        return c
+
+    lax.fori_loop(1, z + 1, pass_k, 0)
+
+    def pass_v(pt):
+        source = z * plane + pt
+        v_column(source, z).wait_recv()
+        columns(lambda zt: v_column(source, zt).start())
+
+    peers(lambda pt: when(z < 3, lambda: pass_v(pt)))
     scale = dim ** (-0.5) * LOG2E
 
     def group(g, masked):
         for u in range(GROUP):
-
-            @pl.when(g * GROUP + u < i)
-            def _():
-                arrival(g * GROUP + u).wait_recv()
-
-        keys = jnp.concatenate([kvbuf[g * GROUP + u, 0:rows, :] for u in range(GROUP)], axis=0)
+            source = g * GROUP + u
+            when((source < i) & (lax.rem(source, plane) != p), lambda: k_plane(source, p).wait_recv())
+            when(
+                (source < i) & ((source // plane != z) | (z == 3)),
+                lambda: v_column(source, z).wait_recv(),
+            )
+        keys = jnp.concatenate([kbuf[g * GROUP + u] for u in range(GROUP)], axis=0)
         halves = [
-            kvbuf[g * GROUP + u, rows + dim * w : rows + dim * (w + 1), :]
+            vbuf[g * GROUP + u, dim * w : dim * (w + 1), :]
             for u in range(GROUP)
             for w in range(rows // dim)
         ]
@@ -108,48 +144,52 @@
             acc[...] = acc[...] * shrink + mixed[:dim]
         m_s[...] = top
 
-    group(first_group, True)
+    group(last, True)
 
     def earlier(t, c):
-        group(first_group - t, False)
-        return c
-
-    lax.fori_loop(1, first_group + 1, earlier, 0)
+        group(last - t, False)
+        return c
+
+    lax.fori_loop(1, last + 1, earlier, 0)
     for head in range(heads):
-        columns = slice(head * rows, (head + 1) * rows)
-        part = acc[:, columns] / l_s[:, columns]
+        columns_here = slice(head * rows, (head + 1) * rows)
+        part = acc[:, columns_here] / l_s[:, columns_here]
         out_ref[:, head * dim : (head + 1) * dim] = part.T.astype(jnp.bfloat16)
-
-    def finish(peer, c):
-        @pl.when(peer > i)
-        def _():
-            push(peer).wait_send()
-
-        return c
-
-    lax.fori_loop(0, seq_count, finish, 0)
-
-
-def attention(kv, q, seq_count, heads, rows, dim):
+    columns(lambda zt: k_column(zt).wait_send())
+    peers(lambda pt: when((z < 3) | (pt > p), lambda: v_plane(pt).wait_send()))
+    peers(lambda pt: when(pt > p, lambda: k_plane(i, pt).wait_send()))
+    columns(lambda zt: v_column(i, zt).wait_send())
+
+    def passed_k(t, c):
+        peers(lambda pt: k_plane((z - t) * plane + p, pt).wait_send())
+        return c
+
+    lax.fori_loop(1, z + 1, passed_k, 0)
+    peers(lambda pt: columns(lambda zt: v_column(z * plane + pt, zt).wait_send()))
+
+
+def attention(k, v, q, seq_count, heads, rows, dim):
     return pl.pallas_call(
-        functools.partial(attention_kernel, seq_count, heads, rows, dim),
+        functools.partial(attention_kernel, heads, rows, dim),
         out_shape=jax.ShapeDtypeStruct((rows, heads * dim), jnp.bfloat16),
-        in_specs=[pl.BlockSpec(memory_space=pltpu.VMEM)] * 2,
+        in_specs=[pl.BlockSpec(memory_space=pltpu.VMEM)] * 3,
         out_specs=pl.BlockSpec(memory_space=pltpu.VMEM),
         scratch_shapes=[
-            pltpu.VMEM((seq_count,) + kv.shape, jnp.bfloat16),
+            pltpu.VMEM((seq_count,) + k.shape, jnp.bfloat16),
+            pltpu.VMEM((seq_count,) + v.shape, jnp.bfloat16),
             pltpu.VMEM((1, heads * rows), jnp.float32),
             pltpu.VMEM((1, heads * rows), jnp.float32),
             pltpu.VMEM((dim, heads * rows), jnp.float32),
+            pltpu.SemaphoreType.DMA((seq_count + 4,)),
+            pltpu.SemaphoreType.DMA((seq_count + 8,)),
             pltpu.SemaphoreType.DMA((seq_count,)),
             pltpu.SemaphoreType.DMA((seq_count,)),
-            pltpu.SemaphoreType.DMA,
         ],
         compiler_params=pltpu.CompilerParams(
             collective_id=0, has_side_effects=True, vmem_limit_bytes=50 << 20
         ),
         name="attention",
-    )(kv, q)
+    )(k, v, q)
 
 
 def cut_along(array, dim, devices):
@@ -450,8 +490,7 @@
     queries = queries.transpose(2, 1, 0).reshape(head_dim, heads_here * tok_rows)
     value_t = value_rows.T.reshape(head_dim, tok_rows // head_dim, head_dim)
     value_t = value_t.transpose(1, 0, 2).reshape(tok_rows, head_dim)
-    kv_block = jnp.concatenate([key_rows, value_t], axis=0)
-    attended = attention(kv_block, queries, seq_count, heads_here, tok_rows, head_dim)
+    attended = attention(key_rows, value_t, queries, seq_count, heads_here, tok_rows, head_dim)
     rows_here = tok_rows // head_count
     own_rows = lax.dynamic_slice_in_dim(tokens, head_index * rows_here, rows_here, 0)
     products = jnp.dot(attended, w_out, preferred_element_type=jnp.float32).astype(jnp.bfloat16)

time: 211 us -> 192 us (0.910)
  Pallas kernels: 173 us -> 156 us
  starting transfers between devices: 6.99 us -> 3.65 us
    pallas_call x1, Pallas kernels: 58.8 us -> 36.3 us  [attention(): pl.pallas_call(functools.partial(attention_kernel, heads, rows, dim), out...]
    pallas_call x1, Pallas kernels: 114 us -> 120 us  [experts(): pl.pallas_call(functools.partial(expert_kernel, cap, chunks), out_shape=j...]
    all_to_all x1, starting transfers between devices: 6.99 us -> 3.65 us  [body(): lax.all_to_all(cut_along(products, 0, head_count), 'head', split_axis=0,...]
where the time goes in v1:
time: 192 us; the launch traced here: 190 us
  Pallas kernels  156 us (81%)
  waiting for transfers between devices  12 us (6%)
  matrix products  9.46 us (5%)
  other arithmetic  5.86 us (3%)
  starting transfers between devices  3.65 us (2%)
  local copies, waits for them, and re-layouts  2.99 us (2%)
    pallas_call x1, Pallas kernels, experts(): pl.pallas_call(functools.partial(expert_kernel, cap, chunks), out_shape=j...  120 us
    pallas_call x1, Pallas kernels, attention(): pl.pallas_call(functools.partial(attention_kernel, heads, rows, dim), out...  36.3 us
    all_to_all x1, waiting for transfers between devices, body(): lax.all_to_all(cut_along(products, 0, head_count), 'head', split_axis=0,...  12 us
    dot_general x1, matrix products, body(): jnp.dot(attended, w_out, preferred_element_type=jnp.float32)  4.43 us
  transfers between devices with their start and end apart: 1, of which 1 were waited for; matrix products, arithmetic and copies ran while one was open for 1% of the time, Pallas kernels for 0%

profile of v1, /device:TPU:2, one launch (start us, length us, event | category | flops | bytes accessed | tf_op | source)
XLA Modules:
  0.0 190.4 jit_solution(2559219434915029860)
XLA Ops:
  0.0 1.6 fusion
  1.6 3.8 %convolution_bitcast_fusion = f32[32,8,8,128]{3,1,2,0:T(8,128)S(1)} fusion(bf16[2048,1024]{1,0:T(8,128)(2,1)} %param.16, bf16[256,2048]{1,0:T(8,128)(2,1)} %param.14, f32[2048]{0:T(1024)} %param.15, f32[256]{0:T(256)S(1)} %add_rsqrt_fusion.2), kind=kOutput, calls=%fused_computation.6 | convolution fusion | flops 1075838976 | bytes 6300672 | tf_op jit(solution)/shard_map/dot_general | solution.py:477
  5.4 0.2 copy.49
  5.6 0.3 multiply_reduce_fusion
  6.1 0.1 copy.47
  6.2 0.3 multiply_multiply_fusion
  6.6 0.5 multiply_cosine_fusion
  7.1 0.5 subtract_convert_fusion
  7.6 0.3 maximum_bitcast_fusion
  7.9 0.6 copy.48
  8.5 0.1 copy.50
  8.7 0.2 copy-done.2
  8.8 0.6 multiply_reduce_fusion.1
  9.4 0.1 copy.44
  9.5 0.1 multiply_bitcast_fusion
  9.6 0.6 fusion.14
  10.2 0.5 convolution_convert_fusion.1
  10.7 0.1 copy.45
  10.9 0.1 pad_maximum_fusion.k_ref
  11.0 36.3 %attention.1 = bf16[256,1024]{1,0:T(8,128)(2,1)S(1)} custom-call(bf16[256,128]{1,0:T(8,128)(2,1)S(1)} %pad_maximum_fusion.k_ref, bf16[256,128]{1,0:T(8,128)(2,1)S(1)} %bitcast.32, bf16[128,2048]{1,0:T(8,128)(2,1)S(1)} %bitcast.31), custom_call_target="tpu_custom_call" | custom-call | tf_op jit(solution)/shard_map/attention/pallas_call | solution.py:172
  47.3 4.4 %convolution_convert_fusion = bf16[256,2048]{1,0:T(8,128)(2,1)} fusion(bf16[256,1024]{1,0:T(8,128)(2,1)S(1)} %attention.1, bf16[1024,2048]{1,0:T(8,128)(2,1)} %param.21), kind=kOutput, calls=%fused_computation.2 | convolution fusion | flops 1074266112 | bytes 5767168 | tf_op jit(solution)/shard_map/dot_general | solution.py:496
  51.7 3.6 %all-to-all-start = ((bf16[4,64,2048]{2,1,0:T(8,128)(2,1)}), bf16[4,64,2048]{2,1,0:T(8,128)(2,1)S(1)}, u32[]{:S(2)}, u32[]{:S(2)}) async-start(bf16[4,64,2048]{2,1,0:T(8,128)(2,1)} %bitcast.39), calls=%async_computation | async-start | bytes 2097152 | tf_op jit(solution)/shard_map/all_to_all | solution.py:497
  55.5 0.2 fusion.3
  55.7 0.1 convolution_convert_fusion.2
  55.9 0.1 copy.40
  56.0 0.1 reshape.188.idx_ref
  56.1 1.2 select_reduce_fusion
  57.5 0.1 reshape.189.slot_ref
  57.7 0.1 reshape.190.mix_ref
  57.9 12.0 %all-to-all-done.part_ref = bf16[4,64,2048]{2,1,0:T(8,128)(2,1)S(1)} async-done(((bf16[4,64,2048]{2,1,0:T(8,128)(2,1)}), bf16[4,64,2048]{2,1,0:T(8,128)(2,1)S(1)}, u32[]{:S(2)}, u32[]{:S(2)}) %all-to-all-start) | async-done | bytes 1048608 | tf_op jit(solution)/shard_map/all_to_all | solution.py:497
  69.8 119.9 %experts.1 = bf16[64,2048]{1,0:T(8,128)(2,1)S(1)} custom-call(s32[768]{0:T(1024)S(1)} %reshape.188.idx_ref, s32[512]{0:T(512)S(1)} %reshape.189.slot_ref, f32[512]{0:T(512)S(1)} %reshape.190.mix_ref, bf16[64,2048]{1,0:T(8,128)(2,1)S(1)} %constant_dynamic-slice_fusion.own_ref, bf16[4,64,2048]{2,1,0:T(8,128)(2,1)S(1)} %all-to-all-done.part_ref, ...), custom_call_target="tpu_custom_call" | custom-call | tf_op jit(solution)/shard_map/experts/pallas_call | solution.py:421
  189.7 0.7 copy.52
  (32 shorter events, 0.6 us)
Async XLA Ops:
  0.0 8.6 %copy-start = (bf16[2048,128]{1,0:T(8,128)(2,1)S(1)}, bf16[2048,128]{1,0:T(8,128)(2,1)}, u32[]{:S(2)}) copy-start(bf16[2048,128]{1,0:T(8,128)(2,1)} %param.17) | copy-start | bytes 1572868
  5.4 0.8 copy-start.5
  7.6 1.2 copy-start.2
  7.6 1.2 copy-start.8
  7.9 1.6 copy-start.6
  8.5 1.7 copy-start.7
  51.7 3.7 %copy-start.3 = (s32[64,8]{0,1:T(8,128)S(1)}, s32[64,8]{0,1:T(8,128)}, u32[]{:S(2)}) copy-start(s32[64,8]{0,1:T(8,128)} %param.23) | copy-start | bytes 6148
  51.7 5.9 %copy-start.4 = (f32[64,8]{0,1:T(8,128)S(1)}, f32[64,8]{0,1:T(8,128)}, u32[]{:S(2)}) copy-start(f32[64,8]{0,1:T(8,128)} %param.24) | copy-start | bytes 6148
  51.7 18.1 %copy-start.1 = (f32[2048]{0:T(1024)S(1)}, f32[2048]{0:T(1024)}, u32[]{:S(2)}) copy-start(f32[2048]{0:T(1024)} %param.22) | copy-start | bytes 24580
  51.7 18.1 %all-to-all-start = ((bf16[4,64,2048]{2,1,0:T(8,128)(2,1)}), bf16[4,64,2048]{2,1,0:T(8,128)(2,1)S(1)}, u32[]{:S(2)}, u32[]{:S(2)}) async-start(bf16[4,64,2048]{2,1,0:T(8,128)(2,1)} %bitcast.39), calls=%async_computation | async-start | bytes 2097152 | tf_op jit(solution)/shard_map/all_to_all | solution.py:497

commit v2 on v1

--- a/solution.py
+++ b/solution.py
@@ -15,15 +15,62 @@
 CAPACITY = 6
 
 
-def attention_kernel(
-    heads, rows, dim, k_ref, v_ref, q_ref, out_ref, kbuf, vbuf, m_s, l_s, acc, send_k, send_v, recv_k, recv_v
+def front_kernel(
+    heads,
+    dim,
+    tok_ref,
+    in_gain,
+    wk_ref,
+    wv_ref,
+    q_gain,
+    k_gain,
+    cos_ref,
+    sin_ref,
+    wq_hbm,
+    wo_hbm,
+    out_ref,
+    wq,
+    wo,
+    normed,
+    q_t,
+    kbuf,
+    vbuf,
+    m_s,
+    l_s,
+    acc,
+    attended,
+    product,
+    kept,
+    pair_out,
+    pair_in,
+    chip_out,
+    chip_in,
+    weight_sem,
+    send_k,
+    send_v,
+    recv_k,
+    recv_v,
+    send_pair,
+    recv_pair,
+    send_chip,
+    recv_chip,
 ):
     i = lax.axis_index("seq")
     h = lax.axis_index("head")
+    rows, width = tok_ref.shape
     count = lax.axis_size("seq")
     plane = count // 4
     z, p = i // plane, lax.rem(i, plane)
     last = i // GROUP
+    y_lo, core = h // 2, lax.rem(h, 2)
+    partner = y_lo * 2 + 1 - core
+    mate = (1 - y_lo) * 2 + core
+    loads = [
+        pltpu.make_async_copy(wq_hbm, wq, weight_sem.at[0]),
+        pltpu.make_async_copy(wo_hbm, wo, weight_sem.at[1]),
+    ]
+    for load in loads:
+        load.start()
     for u in range(GROUP):
 
         @pl.when(last * GROUP + u > i)
@@ -31,8 +78,6 @@
             kbuf[last * GROUP + u] = jnp.zeros(kbuf.shape[1:], kbuf.dtype)
             vbuf[last * GROUP + u] = jnp.zeros(vbuf.shape[1:], vbuf.dtype)
 
-    kbuf[i] = k_ref[...]
-    vbuf[i] = v_ref[...]
     barrier = pltpu.get_barrier_semaphore()
 
     def greet(t, c):
@@ -42,7 +87,23 @@
         return c
 
     lax.fori_loop(1, count, greet, 0)
-    pl.semaphore_wait(barrier, count - 1)
+    for other in (partner, mate):
+        pl.semaphore_signal(barrier, inc=1, device_id=(i, other), device_id_type=MESH)
+
+    def turned(vectors, gain):
+        mean_sq = jnp.mean(vectors * vectors, axis=-1, keepdims=True)
+        vectors = vectors * lax.rsqrt(mean_sq + EPSILON) * gain
+        return vectors * cos_ref[...] + pltpu.roll(vectors, dim // 2, 1) * sin_ref[...]
+
+    tokens = tok_ref[...].astype(jnp.float32)
+    mean_sq = jnp.mean(tokens * tokens, axis=-1, keepdims=True)
+    normed[...] = (tokens * lax.rsqrt(mean_sq + EPSILON) * in_gain[...]).astype(jnp.bfloat16)
+    key = jnp.dot(normed[...], wk_ref[...], preferred_element_type=jnp.float32)
+    kbuf[i] = turned(key, k_gain[...]).astype(jnp.bfloat16)
+    value = jnp.dot(normed[...], wv_ref[...], preferred_element_type=jnp.float32)
+    for w in range(rows // dim):
+        vbuf[i, dim * w : dim * (w + 1), :] = value[dim * w : dim * (w + 1)].T.astype(jnp.bfloat16)
+    pl.semaphore_wait(barrier, count + 1)
 
     def copy(buf, send, recv, at, source, zt, pt):
         return pltpu.make_async_remote_copy(
@@ -66,9 +127,6 @@
     def v_column(source, zt):
         return copy(vbuf, send_v, recv_v, lax.rem(source, plane) * 4 + zt, source, zt, p)
 
-    def peer(t):
-        return lax.rem(p + t, plane)
-
     def columns(act):
         def one(zt, c):
             act(zt)
@@ -78,7 +136,7 @@
 
     def peers(act):
         def one(t, c):
-            act(peer(t))
+            act(lax.rem(p + t, plane))
             return c
 
         lax.fori_loop(1, plane, one, 0)
@@ -92,6 +150,15 @@
     peers(lambda pt: when((z < 3) | (pt > p), lambda: v_plane(pt).start()))
     peers(lambda pt: when(pt > p, lambda: k_plane(i, pt).start()))
     columns(lambda zt: v_column(i, zt).start())
+    loads[0].wait()
+    for two in range(heads // 2):
+        both = jnp.dot(
+            normed[...], wq[:, two * 2 * dim : (two + 1) * 2 * dim], preferred_element_type=jnp.float32
+        )
+        for w in range(2):
+            head = two * 2 + w
+            query = turned(both[:, w * dim : (w + 1) * dim], q_gain[...])
+            q_t[:, head * rows : (head + 1) * rows] = query.T.astype(jnp.bfloat16)
 
     def pass_k(t, c):
         source = (z - t) * plane + p
@@ -125,7 +192,7 @@
         ]
         values = jnp.concatenate(halves, axis=1)
         values = jnp.concatenate([values, jnp.ones((16, values.shape[1]), values.dtype)], axis=0)
-        scores = jnp.dot(keys, q_ref[...], preferred_element_type=jnp.float32)
+        scores = jnp.dot(keys, q_t[...], preferred_element_type=jnp.float32)
         if masked:
             key_at = lax.broadcasted_iota(jnp.int32, scores.shape, 0)
             query_at = lax.broadcasted_iota(jnp.int32, scores.shape, 1) % rows + (i - g * GROUP) * rows
@@ -154,7 +221,63 @@
     for head in range(heads):
         columns_here = slice(head * rows, (head + 1) * rows)
         part = acc[:, columns_here] / l_s[:, columns_here]
-        out_ref[:, head * dim : (head + 1) * dim] = part.T.astype(jnp.bfloat16)
+        attended[:, head * dim : (head + 1) * dim] = part.T.astype(jnp.bfloat16)
+    loads[1].wait()
+    chunks = pair_out.shape[0]
+    wide = width // chunks
+    own = rows // 4
+
+    def block(r):
+        return pl.ds(pl.multiple_of(r * own, own), own)
+
+    def to_partner(n):
+        return pltpu.make_async_remote_copy(
+            src_ref=pair_out.at[n],
+            dst_ref=pair_in.at[n],
+            send_sem=send_pair.at[n],
+            recv_sem=recv_pair.at[n],
+            device_id=(i, partner),
+            device_id_type=MESH,
+        )
+
+    def to_mate(n):
+        return pltpu.make_async_remote_copy(
+            src_ref=chip_out.at[n],
+            dst_ref=chip_in.at[n],
+            send_sem=send_chip.at[n],
+            recv_sem=recv_chip.at[n],
+            device_id=(i, mate),
+            device_id_type=MESH,
+        )
+
+    def sum_pair(n):
+        at = slice(n * wide, (n + 1) * wide)
+        to_partner(n).wait_recv()
+        far = kept[pl.ds(pl.multiple_of((1 - y_lo) * own, own), own), at]
+        far = far + pair_in[n, pl.ds(pl.multiple_of((1 - y_lo) * own, own), own), :].astype(jnp.float32)
+        chip_out[n] = far.astype(jnp.bfloat16)
+        to_mate(n).start()
+        near = kept[pl.ds(pl.multiple_of(y_lo * own, own), own), at]
+        near = near + pair_in[n, pl.ds(pl.multiple_of(y_lo * own, own), own), :].astype(jnp.float32)
+        out_ref[:, at] = near + tok_ref[block(h), at].astype(jnp.float32)
+
+    for n in range(chunks):
+        at = slice(n * wide, (n + 1) * wide)
+        product[...] = jnp.dot(attended[...], wo[:, at], preferred_element_type=jnp.float32)
+        for half in range(2):
+            pair_out[n, half * own : (half + 1) * own, :] = product[
+                block(half * 2 + 1 - core), :
+            ].astype(jnp.bfloat16)
+        to_partner(n).start()
+        for half in range(2):
+            kept[half * own : (half + 1) * own, at] = product[block(half * 2 + core), :]
+        if n > 0:
+            sum_pair(n - 1)
+    sum_pair(chunks - 1)
+    for n in range(chunks):
+        at = slice(n * wide, (n + 1) * wide)
+        to_mate(n).wait_recv()
+        out_ref[:, at] = out_ref[:, at] + chip_in[n].astype(jnp.float32)
     columns(lambda zt: k_column(zt).wait_send())
     peers(lambda pt: when((z < 3) | (pt > p), lambda: v_plane(pt).wait_send()))
     peers(lambda pt: when(pt > p, lambda: k_plane(i, pt).wait_send()))
@@ -166,58 +289,57 @@
 
     lax.fori_loop(1, z + 1, passed_k, 0)
     peers(lambda pt: columns(lambda zt: v_column(z * plane + pt, zt).wait_send()))
-
-
-def attention(k, v, q, seq_count, heads, rows, dim):
+    for n in range(chunks):
+        to_partner(n).wait_send()
+        to_mate(n).wait_send()
+
+
+def front(tokens, in_gain, wk, wv, q_gain, k_gain, cosine, sine, wq, wo, seq_count):
+    rows, width = tokens.shape
+    dim = wk.shape[1]
+    heads = wq.shape[1] // dim
+    own = rows // 4
+    chunks = 4
+    wide = width // chunks
+    vmem = pl.BlockSpec(memory_space=pltpu.VMEM)
+    hbm = pl.BlockSpec(memory_space=pl.ANY)
     return pl.pallas_call(
-        functools.partial(attention_kernel, heads, rows, dim),
-        out_shape=jax.ShapeDtypeStruct((rows, heads * dim), jnp.bfloat16),
-        in_specs=[pl.BlockSpec(memory_space=pltpu.VMEM)] * 3,
-        out_specs=pl.BlockSpec(memory_space=pltpu.VMEM),
+        functools.partial(front_kernel, heads, dim),
+        out_shape=jax.ShapeDtypeStruct((own, width), jnp.float32),
+        in_specs=[vmem] * 8 + [hbm] * 2,
+        out_specs=vmem,
         scratch_shapes=[
-            pltpu.VMEM((seq_count,) + k.shape, jnp.bfloat16),
-            pltpu.VMEM((seq_count,) + v.shape, jnp.bfloat16),
+            pltpu.VMEM(wq.shape, jnp.bfloat16),
+            pltpu.VMEM(wo.shape, jnp.bfloat16),
+            pltpu.VMEM(tokens.shape, jnp.bfloat16),
+            pltpu.VMEM((dim, heads * rows), jnp.bfloat16),
+            pltpu.VMEM((seq_count, rows, dim), jnp.bfloat16),
+            pltpu.VMEM((seq_count, rows, dim), jnp.bfloat16),
             pltpu.VMEM((1, heads * rows), jnp.float32),
             pltpu.VMEM((1, heads * rows), jnp.float32),
             pltpu.VMEM((dim, heads * rows), jnp.float32),
+            pltpu.VMEM((rows, heads * dim), jnp.bfloat16),
+            pltpu.VMEM((rows, wide), jnp.float32),
+            pltpu.VMEM((2 * own, width), jnp.float32),
+            pltpu.VMEM((chunks, 2 * own, wide), jnp.bfloat16),
+            pltpu.VMEM((chunks, 2 * own, wide), jnp.bfloat16),
+            pltpu.VMEM((chunks, own, wide), jnp.bfloat16),
+            pltpu.VMEM((chunks, own, wide), jnp.bfloat16),
+            pltpu.SemaphoreType.DMA((2,)),
             pltpu.SemaphoreType.DMA((seq_count + 4,)),
             pltpu.SemaphoreType.DMA((seq_count + 8,)),
             pltpu.SemaphoreType.DMA((seq_count,)),
             pltpu.SemaphoreType.DMA((seq_count,)),
+            pltpu.SemaphoreType.DMA((chunks,)),
+            pltpu.SemaphoreType.DMA((chunks,)),
+            pltpu.SemaphoreType.DMA((chunks,)),
+            pltpu.SemaphoreType.DMA((chunks,)),
         ],
         compiler_params=pltpu.CompilerParams(
             collective_id=0, has_side_effects=True, vmem_limit_bytes=50 << 20
         ),
-        name="attention",
-    )(k, v, q)
-
-
-def cut_along(array, dim, devices):
-    dims = array.shape
-    blocks = array.reshape(*dims[:dim], devices, dims[dim] // devices, *dims[dim + 1 :])
-    return jnp.moveaxis(blocks, dim, 0)
-
-
-def rms_scale(vectors, gain_vector):
-    mean_sq = jnp.mean(vectors * vectors, axis=-1, keepdims=True)
-    return vectors * lax.rsqrt(mean_sq + EPSILON) * gain_vector
-
-
-def rotate(vectors, positions):
-    half_dim = vectors.shape[-1] // 2
-    frequency = THETA ** (-jnp.arange(half_dim, dtype=jnp.float32) * 2.0 / vectors.shape[-1])
-    angles = positions[:, None] * frequency[None, :]
-    cosine_table = jnp.cos(angles)[:, None, :]
-    sine_table = jnp.sin(angles)[:, None, :]
-    front_half = vectors[..., :half_dim]
-    back_half = vectors[..., half_dim:]
-    return jnp.concatenate(
-        [
-            front_half * cosine_table - back_half * sine_table,
-            back_half * cosine_table + front_half * sine_table,
-        ],
-        axis=-1,
-    )
+        name="front",
+    )(tokens, in_gain, wk, wv, q_gain, k_gain, cosine, sine, wq, wo)
 
 
 def neighbour(s, h, step, sign):
@@ -237,7 +359,6 @@
     slot_ref,
     mix_ref,
     own_ref,
-    part_ref,
     gain_ref,
     gate_hbm,
     up_hbm,
@@ -279,9 +400,7 @@
     ]
     for load in loads:
         load.start()
-    residual = own_ref[...].astype(jnp.float32)
-    for n in range(part_ref.shape[0]):
-        residual = residual + part_ref[n].astype(jnp.float32)
+    residual = own_ref[...]
     mean_sq = jnp.mean(residual * residual, axis=-1, keepdims=True)
     routed = residual * lax.rsqrt(mean_sq + EPSILON) * gain_ref[...]
     span = rows * cuts
@@ -407,7 +526,7 @@
     lax.fori_loop(1, count, finish, 0)
 
 
-def experts(idx, slot, mix, own, parts, gain, w_gate, w_up, w_down, cap):
+def experts(idx, slot, mix, own, gain, w_gate, w_up, w_down, cap):
     rows, width = own.shape
     depth, hidden = w_gate.shape
     cuts = width // 128
@@ -421,7 +540,7 @@
     return pl.pallas_call(
         functools.partial(expert_kernel, cap, chunks),
         out_shape=jax.ShapeDtypeStruct((rows, width), jnp.bfloat16),
-        in_specs=[smem, smem, smem, vmem, vmem, vmem, hbm, hbm, hbm],
+        in_specs=[smem, smem, smem, vmem, vmem, hbm, hbm, hbm],
         out_specs=vmem,
         scratch_shapes=[
             pltpu.VMEM((depth, hidden), jnp.bfloat16),
@@ -445,7 +564,7 @@
             collective_id=1, has_side_effects=True, vmem_limit_bytes=50 << 20
         ),
         name="experts",
-    )(idx, slot, mix, own, parts, gain, w_gate, w_up, w_down)
+    )(idx, slot, mix, own, gain, w_gate, w_up, w_down)
 
 
 def body(
@@ -464,39 +583,29 @@
     w_up,
     w_down,
 ):
-    tok_rows, width = tokens.shape
+    tok_rows = tokens.shape[0]
     head_dim = query_gain.shape[0]
-    heads_here = w_query.shape[1] // head_dim
     seq_count = lax.axis_size("seq")
-    seq_index = lax.axis_index("seq")
     head_count = lax.axis_size("head")
-    head_index = lax.axis_index("head")
-    normed = rms_scale(tokens.astype(jnp.float32), input_gain).astype(jnp.bfloat16)
-    offset = seq_index * tok_rows
-    positions = (offset + jnp.arange(tok_rows, dtype=jnp.int32)).astype(jnp.float32)
-    queries = jnp.dot(normed, w_query, preferred_element_type=jnp.float32).reshape(
-        tok_rows, heads_here, head_dim
+    half_dim = head_dim // 2
+    positions = (lax.axis_index("seq") * tok_rows + jnp.arange(tok_rows, dtype=jnp.int32)).astype(jnp.float32)
+    frequency = THETA ** (-jnp.arange(half_dim, dtype=jnp.float32) * 2.0 / head_dim)
+    angles = positions[:, None] * frequency[None, :]
+    cosine, sine = jnp.cos(angles), jnp.sin(angles)
+    residual = front(
+        tokens,
+        input_gain.reshape(1, -1),
+        w_key,
+        w_value,
+        query_gain.reshape(1, -1),
+        key_gain.reshape(1, -1),
+        jnp.concatenate([cosine, cosine], axis=1),
+        jnp.concatenate([-sine, sine], axis=1),
+        w_query,
+        w_out,
+        seq_count,
     )
-    queries = rotate(rms_scale(queries, query_gain), positions).astype(jnp.bfloat16)
-    key_rows = jnp.dot(normed, w_key, preferred_element_type=jnp.float32).reshape(
-        tok_rows, 1, head_dim
-    )
-    key_rows = (
-        rotate(rms_scale(key_rows, key_gain), positions)
-        .astype(jnp.bfloat16)
-        .reshape(tok_rows, head_dim)
-    )
-    value_rows = jnp.dot(normed, w_value, preferred_element_type=jnp.float32).astype(jnp.bfloat16)
-    queries = queries.transpose(2, 1, 0).reshape(head_dim, heads_here * tok_rows)
-    value_t = value_rows.T.reshape(head_dim, tok_rows // head_dim, head_dim)
-    value_t = value_t.transpose(1, 0, 2).reshape(tok_rows, head_dim)
-    attended = attention(key_rows, value_t, queries, seq_count, heads_here, tok_rows, head_dim)
-    rows_here = tok_rows // head_count
-    own_rows = lax.dynamic_slice_in_dim(tokens, head_index * rows_here, rows_here, 0)
-    products = jnp.dot(attended, w_out, preferred_element_type=jnp.float32).astype(jnp.bfloat16)
-    parts = lax.all_to_all(
-        cut_along(products, 0, head_count), "head", split_axis=0, concat_axis=0, tiled=True
-    )
+    rows_here = residual.shape[0]
     experts_all = w_gate.shape[0] * seq_count * head_count
     top_count = expert_ids.shape[1]
     onehot = expert_ids[:, :, None] == jnp.arange(experts_all, dtype=jnp.int32)
@@ -512,8 +621,7 @@
         idx.reshape(-1),
         slot.reshape(-1),
         mixing.reshape(-1),
-        own_rows,
-        parts,
+        residual,
         post_gain.reshape(1, -1),
         w_gate[0],
         w_up[0],

time: 192 us -> 180 us (0.938)
  waiting for transfers between devices: 12 us -> 0 us
  Pallas kernels: 156 us -> 166 us
  matrix products: 9.46 us -> 0.13 us
  local copies, waits for them, and re-layouts: 2.99 us -> 7.46 us
  starting transfers between devices: 3.65 us -> 0 us
    all_to_all x1 -> x0, waiting for transfers between devices: 12 us -> none  [body(): lax.all_to_all(cut_along(products, 0, head_count), 'head', split_axis=0,...]
    pallas_call x1, Pallas kernels: 120 us -> 130 us  [experts(): pl.pallas_call(functools.partial(expert_kernel, cap, chunks), out_shape=j...]
    dot_general x4 -> x0, matrix products: 9.33 us -> none  [the longest x1 4.43 us: body(): jnp.dot(attended, w_out, preferred_element_type=jnp.float32)]
    unnamed x22 -> x18, local copies, waits for them, and re-layouts: 1.32 us -> 6.79 us
    all_to_all x1 -> x0, starting transfers between devices: 3.65 us -> none  [body(): lax.all_to_all(cut_along(products, 0, head_count), 'head', split_axis=0,...]
  transfers between devices with their start and end apart: 1 -> 0, of which waited for: 1 -> 0; matrix products, arithmetic and copies ran while one was open for 1% -> 0% of each run, Pallas kernels for 0% -> 0%
where the time goes in v2:
time: 180 us; the launch traced here: 178 us
  Pallas kernels  166 us (92%)
  local copies, waits for them, and re-layouts  7.46 us (4%)
  other arithmetic  4.25 us (2%)
    pallas_call x1, Pallas kernels, experts(): pl.pallas_call(functools.partial(expert_kernel, cap, chunks), out_shape=j...  130 us
    pallas_call x1, Pallas kernels, front(): pl.pallas_call(functools.partial(front_kernel, heads, dim), out_shape=jax...  36.2 us
    unnamed x18, local copies, waits for them, and re-layouts  6.79 us

profile of v2, /device:TPU:2, one launch (start us, length us, event | category | flops | bytes accessed | tf_op | source)
XLA Modules:
  0.0 177.9 jit_solution(11528652564933536210)
XLA Ops:
  0.0 0.7 reduce_sum.29
  0.7 0.7 broadcast_divide_fusion
  1.4 0.1 copy.28
  1.5 0.1 reshape.39.mix_ref
  1.6 0.8 copy.24
  2.4 0.2 fusion
  2.5 0.1 convolution_convert_fusion
  2.7 0.1 select_reduce_fusion.1
  2.7 1.2 select_reduce_fusion
  4.0 0.1 copy.26
  4.0 0.7 multiply_add_fusion
  4.7 0.1 copy.27
  4.8 0.1 reshape.38.slot_ref
  4.9 0.1 copy.25
  5.0 0.1 reshape.37.idx_ref
  5.2 0.5 fusion.2
  5.7 0.1 pad_maximum_fusion
  5.9 0.0 copy-start.1
  5.9 1.2 copy-done.1
  7.1 0.0 copy-start.2
  7.1 1.0 copy-done.2
  8.1 0.0 copy-start.3
  8.1 1.0 copy-done.3
  9.2 0.0 copy-start.4
  9.2 0.7 copy-done.4
  9.9 0.7 copy-done.6
  10.5 0.7 copy-done.7
  11.2 36.2 %front.1.own_ref = f32[64,2048]{1,0:T(8,128)S(1)} custom-call(bf16[256,2048]{1,0:T(8,128)(2,1)S(1)} %copy-done.1, f32[1,2048]{1,0:T(1,128)S(1)} %bitcast.9, bf16[2048,128]{1,0:T(8,128)(2,1)S(1)} %copy-done.2, bf16[2048,128]{1,0:T(8,128)(2,1)S(1)} %copy-done.3, f32[1,128]{1,0:T(1,128)S(1)} %bitcast.11, f32[1,128]{1,0:T(1,128)S(1)} %bitcast.12, ...), custom_call_target="tpu_custom_call" | custom-call | tf_op jit(solution)/shard_map/front/pallas_call | solution.py:306
  47.4 0.0 copy-done
  47.4 0.0 copy-done.5
  47.4 129.8 %experts.1 = bf16[64,2048]{1,0:T(8,128)(2,1)S(1)} custom-call(s32[768]{0:T(1024)S(1)} %reshape.37.idx_ref, s32[512]{0:T(512)S(1)} %reshape.38.slot_ref, f32[512]{0:T(512)S(1)} %reshape.39.mix_ref, f32[64,2048]{1,0:T(8,128)S(1)} %front.1.own_ref, f32[1,2048]{1,0:T(1,128)S(1)} %bitcast.10, bf16[2048,768]{1,0:T(8,128)(2,1)S(1)} %bitcast.8, ...), custom_call_target="tpu_custom_call" | custom-call | tf_op jit(solution)/shard_map/experts/pallas_call | solution.py:540
  177.2 0.7 copy.30
  (6 shorter events, 0.0 us)
Async XLA Ops:
  5.9 1.2 copy-start.1
  7.1 1.0 copy-start.2
  8.1 1.0 copy-start.3
  9.2 0.7 copy-start.4
  9.9 0.7 copy-start.6
  10.5 0.7 copy-start.7
  11.2 36.2 %copy-start = (bf16[1,2048,768]{2,1,0:T(8,128)(2,1)S(1)}, bf16[1,2048,768]{2,1,0:T(8,128)(2,1)}, u32[]{:S(2)}) copy-start(bf16[1,2048,768]{2,1,0:T(8,128)(2,1)} %param.25) | copy-start | bytes 9437188
  11.2 36.2 %copy-start.5 = (f32[2048]{0:T(1024)S(1)}, f32[2048]{0:T(1024)}, u32[]{:S(2)}) copy-start(f32[2048]{0:T(1024)} %param.22) | copy-start | bytes 24580

commit v3 on v2

v3 whole, which is shorter than its diff:
```python
import functools

import jax
import jax.numpy as jnp
from jax import lax
from jax.experimental import pallas as pl
from jax.experimental.pallas import tpu as pltpu
from jax.sharding import PartitionSpec as P

MESH = pl.DeviceIdType.MESH
EPSILON = 1e-06
THETA = 1000000.0
LOG2E = 1.4426950408889634
GROUP = 4
CAPACITY = 6


def neighbour(s, h, step):
    z, x, y, core = s // 8, lax.rem(s // 2, 4), lax.rem(s, 2) * 2 + h // 2, lax.rem(h, 2)
    turn = lax.rem(step * 37, 128)
    z = lax.rem(z + turn // 32, 4)
    x = lax.rem(x + lax.rem(turn // 8, 4), 4)
    y = lax.rem(y + lax.rem(turn // 2, 4), 4)
    core = lax.rem(core + lax.rem(turn, 2), 2)
    return z * 8 + x * 2 + y // 2, lax.rem(y, 2) * 2 + core


def layer_kernel(
    heads,
    dim,
    cap,
    in_gain,
    post_gain,
    q_gain,
    k_gain,
    cos_ref,
    sin_ref,
    ids_ref,
    score_ref,
    tok_hbm,
    wk_hbm,
    wv_hbm,
    wq_hbm,
    wo_hbm,
    gate_hbm,
    up_hbm,
    down_hbm,
    out_ref,
    tok_ref,
    wk_ref,
    wv_ref,
    wq,
    wo,
    up,
    normed,
    q_t,
    kbuf,
    vbuf,
    m_s,
    l_s,
    acc,
    attended,
    product,
    kept,
    pair_out,
    pair_in,
    chip_out,
    chip_in,
    residual,
    slot_v,
    mix_v,
    idx_v,
    slot_s,
    mix_s,
    idx_s,
    wide_rows,
    home,
    tiles,
    outgoing,
    arrived,
    batch,
    returned,
    load_sem,
    send_k,
    send_v,
    recv_k,
    recv_v,
    send_pair,
    recv_pair,
    send_chip,
    recv_chip,
    send_out,
    recv_out,
    send_back,
    recv_back,
):
    i = lax.axis_index("seq")
    h = lax.axis_index("head")
    rows, width = tok_ref.shape
    own = rows // 4
    count = lax.axis_size("seq")
    plane = count // 4
    z, p = i // plane, lax.rem(i, plane)
    last = i // GROUP
    y_lo, core = h // 2, lax.rem(h, 2)
    partner = y_lo * 2 + 1 - core
    mate = (1 - y_lo) * 2 + core
    me = i * 4 + h
    devices = count * 4
    hidden_width = up.shape[1]
    gate, down = wq.at[:, 0:hidden_width], wo.at[0:hidden_width, :]

    def load(hbm, vmem, n):
        return pltpu.make_async_copy(hbm, vmem, load_sem.at[n])

    first_loads = [
        load(tok_hbm, tok_ref, 0),
        load(wk_hbm, wk_ref, 1),
        load(wv_hbm, wv_ref, 2),
        load(wq_hbm, wq, 3),
        load(wo_hbm, wo, 4),
        load(up_hbm, up, 5),
    ]
    for one in first_loads:
        one.start()
    for u in range(GROUP):

        @pl.when(last * GROUP + u > i)
        def _():
            kbuf[last * GROUP + u] = jnp.zeros(kbuf.shape[1:], kbuf.dtype)
            vbuf[last * GROUP + u] = jnp.zeros(vbuf.shape[1:], vbuf.dtype)

    barrier = pltpu.get_barrier_semaphore()

    def greet(t, c):
        other = lax.rem(me + t, devices)
        pl.semaphore_signal(
            barrier, inc=1, device_id=(other // 4, lax.rem(other, 4)), device_id_type=MESH
        )
        return c

    lax.fori_loop(1, devices, greet, 0)

    def turned(vectors, gain):
        mean_sq = jnp.mean(vectors * vectors, axis=-1, keepdims=True)
        vectors = vectors * lax.rsqrt(mean_sq + EPSILON) * gain
        return vectors * cos_ref[...] + pltpu.roll(vectors, dim // 2, 1) * sin_ref[...]

    first_loads[0].wait()
    tokens = tok_ref[...].astype(jnp.float32)
    mean_sq = jnp.mean(tokens * tokens, axis=-1, keepdims=True)
    normed[...] = (tokens * lax.rsqrt(mean_sq + EPSILON) * in_gain[...]).astype(jnp.bfloat16)
    first_loads[1].wait()
    key = jnp.dot(normed[...], wk_ref[...], preferred_element_type=jnp.float32)
    kbuf[i] = turned(key, k_gain[...]).astype(jnp.bfloat16)
    first_loads[2].wait()
    value = jnp.dot(normed[...], wv_ref[...], preferred_element_type=jnp.float32)
    for w in range(rows // dim):
        vbuf[i, dim * w : dim * (w + 1), :] = value[dim * w : dim * (w + 1)].T.astype(jnp.bfloat16)
    pl.semaphore_wait(barrier, devices - 1)

    def copy(buf, send, recv, at, source, zt, pt):
        return pltpu.make_async_remote_copy(
            src_ref=buf.at[source],
            dst_ref=buf.at[source],
            send_sem=send.at[at],
            recv_sem=recv.at[source],
            device_id=(zt * plane + pt, h),
            device_id_type=MESH,
        )

    def k_column(zt):
        return copy(kbuf, send_k, recv_k, count + zt, i, zt, p)

    def k_plane(source, pt):
        return copy(kbuf, send_k, recv_k, source // plane * plane + pt, source, z, pt)

    def v_plane(pt):
        return copy(vbuf, send_v, recv_v, count + pt, i, z, pt)

    def v_column(source, zt):
        return copy(vbuf, send_v, recv_v, lax.rem(source, plane) * 4 + zt, source, zt, p)

    def columns(act):
        def one(zt, c):
            act(zt)
            return c

        lax.fori_loop(z + 1, 4, one, 0)

    def peers(act):
        def one(t, c):
            act(lax.rem(p + t, plane))
            return c

        lax.fori_loop(1, plane, one, 0)

    def when(cond, act):
        @pl.when(cond)
        def _():
            act()

    columns(lambda zt: k_column(zt).start())
    peers(lambda pt: when((z < 3) | (pt > p), lambda: v_plane(pt).start()))
    peers(lambda pt: when(pt > p, lambda: k_plane(i, pt).start()))
    columns(lambda zt: v_column(i, zt).start())
    first_loads[3].wait()
    for two in range(heads // 2):
        both = jnp.dot(
            normed[...], wq[:, two * 2 * dim : (two + 1) * 2 * dim], preferred_element_type=jnp.float32
        )
        for w in range(2):
            head = two * 2 + w
            query = turned(both[:, w * dim : (w + 1) * dim], q_gain[...])
            q_t[:, head * rows : (head + 1) * rows] = query.T.astype(jnp.bfloat16)

    load(gate_hbm, gate, 3).start()
    ids = ids_ref[...]
    lane = lax.broadcasted_iota(jnp.int32, (own, devices), 1)
    hits = [ids[:, n : n + 1] == lane for n in range(ids.shape[1])]
    named = sum(jnp.where(hit, 1.0, 0.0) for hit in hits)
    order = [lax.broadcasted_iota(jnp.int32, (own, own), n) for n in range(2)]
    earlier_rows = jnp.where(order[0] > order[1], 1.0, 0.0).astype(jnp.bfloat16)
    rank = jnp.dot(earlier_rows, named.astype(jnp.bfloat16), preferred_element_type=jnp.float32)
    scores_in = score_ref[...]
    mixing = scores_in / jnp.sum(scores_in, axis=1, keepdims=True)
    slots = jnp.zeros((own, devices), jnp.int32)
    mixes = jnp.zeros((own, devices), jnp.float32)
    for n, hit in enumerate(hits):
        place = jnp.sum(jnp.where(hit, rank, 0.0), axis=1, keepdims=True).astype(jnp.int32)
        slots = jnp.where(lane == n, ids[:, n : n + 1] * cap + place, slots)
        mixes = jnp.where(lane == n, mixing[:, n : n + 1], mixes)
    slot_v[...] = slots
    mix_v[...] = mixes
    idx_v[...] = jnp.zeros(idx_v.shape, jnp.int32)
    token_at = lax.broadcasted_iota(jnp.int32, (own, devices), 0).astype(jnp.float32)
    for c in range(cap):
        chosen = (rank == c) & (named > 0)
        row = jnp.sum(jnp.where(chosen, token_at, 0.0), axis=0, keepdims=True)
        idx_v[c : c + 1, :] = row.astype(jnp.int32)
    tables = [load(slot_v, slot_s, 6), load(mix_v, mix_s, 7), load(idx_v, idx_s, 8)]
    for one in tables:
        one.start()

    def pass_k(t, c):
        source = (z - t) * plane + p
        k_plane(source, p).wait_recv()
        peers(lambda pt: k_plane(source, pt).start())
        return c

    lax.fori_loop(1, z + 1, pass_k, 0)

    def pass_v(pt):
        source = z * plane + pt
        v_column(source, z).wait_recv()
        columns(lambda zt: v_column(source, zt).start())

    peers(lambda pt: when(z < 3, lambda: pass_v(pt)))
    scale = dim ** (-0.5) * LOG2E

    def group(g, masked):
        for u in range(GROUP):
            source = g * GROUP + u
            when((source < i) & (lax.rem(source, plane) != p), lambda: k_plane(source, p).wait_recv())
            when(
                (source < i) & ((source // plane != z) | (z == 3)),
                lambda: v_column(source, z).wait_recv(),
            )
        keys = jnp.concatenate([kbuf[g * GROUP + u] for u in range(GROUP)], axis=0)
        halves = [
            vbuf[g * GROUP + u, dim * w : dim * (w + 1), :]
            for u in range(GROUP)
            for w in range(rows // dim)
        ]
        values = jnp.concatenate(halves, axis=1)
        values = jnp.concatenate([values, jnp.ones((16, values.shape[1]), values.dtype)], axis=0)
        scores = jnp.dot(keys, q_t[...], preferred_element_type=jnp.float32)
        if masked:
            key_at = lax.broadcasted_iota(jnp.int32, scores.shape, 0)
            query_at = lax.broadcasted_iota(jnp.int32, scores.shape, 1) % rows + (i - g * GROUP) * rows
            scores = jnp.where(key_at <= query_at, scores, -1e30)
        top = jnp.max(scores, axis=0, keepdims=True)
        if not masked:
            top = jnp.maximum(top, m_s[...])
        weights = jnp.exp2(scores * scale - top * scale)
        mixed = jnp.dot(values, weights.astype(jnp.bfloat16), preferred_element_type=jnp.float32)
        if masked:
            l_s[...] = mixed[dim : dim + 1]
            acc[...] = mixed[:dim]
        else:
            shrink = jnp.exp2((m_s[...] - top) * scale)
            l_s[...] = l_s[...] * shrink + mixed[dim : dim + 1]
            acc[...] = acc[...] * shrink + mixed[:dim]
        m_s[...] = top

    group(last, True)

    def earlier(t, c):
        group(last - t, False)
        return c

    lax.fori_loop(1, last + 1, earlier, 0)
    for head in range(heads):
        columns_here = slice(head * rows, (head + 1) * rows)
        part = acc[:, columns_here] / l_s[:, columns_here]
        attended[:, head * dim : (head + 1) * dim] = part.T.astype(jnp.bfloat16)
    first_loads[4].wait()
    chunks = pair_out.shape[0]
    wide = width // chunks

    def block(r):
        return pl.ds(pl.multiple_of(r * own, own), own)

    def to_partner(n):
        return pltpu.make_async_remote_copy(
            src_ref=pair_out.at[n],
            dst_ref=pair_in.at[n],
            send_sem=send_pair.at[n],
            recv_sem=recv_pair.at[n],
            device_id=(i, partner),
            device_id_type=MESH,
        )

    def to_mate(n):
        return pltpu.make_async_remote_copy(
            src_ref=chip_out.at[n],
            dst_ref=chip_in.at[n],
            send_sem=send_chip.at[n],
            recv_sem=recv_chip.at[n],
            device_id=(i, mate),
            device_id_type=MESH,
        )

    def sum_pair(n):
        at = slice(n * wide, (n + 1) * wide)
        to_partner(n).wait_recv()
        far = kept[pl.ds(pl.multiple_of((1 - y_lo) * own, own), own), at]
        far = far + pair_in[n, pl.ds(pl.multiple_of((1 - y_lo) * own, own), own), :].astype(jnp.float32)
        chip_out[n] = far.astype(jnp.bfloat16)
        to_mate(n).start()
        near = kept[pl.ds(pl.multiple_of(y_lo * own, own), own), at]
        near = near + pair_in[n, pl.ds(pl.multiple_of(y_lo * own, own), own), :].astype(jnp.float32)
        residual[:, at] = near + tok_ref[block(h), at].astype(jnp.float32)

    for n in range(chunks):
        at = slice(n * wide, (n + 1) * wide)
        product[...] = jnp.dot(attended[...], wo[:, at], preferred_element_type=jnp.float32)
        for half in range(2):
            pair_out[n, half * own : (half + 1) * own, :] = product[
                block(half * 2 + 1 - core), :
            ].astype(jnp.bfloat16)
        to_partner(n).start()
        for half in range(2):
            kept[half * own : (half + 1) * own, at] = product[block(half * 2 + core), :]
        if n > 0:
            sum_pair(n - 1)
    sum_pair(chunks - 1)
    for n in range(chunks):
        at = slice(n * wide, (n + 1) * wide)
        to_mate(n).wait_recv()
        residual[:, at] = residual[:, at] + chip_in[n].astype(jnp.float32)
    load(down_hbm, down, 4).start()
    cuts = width // 128
    mean_sq = jnp.mean(residual[...] * residual[...], axis=-1, keepdims=True)
    scale_rows = lax.rsqrt(mean_sq + EPSILON)
    for c in range(cuts):
        at = slice(c * 128, (c + 1) * 128)
        home[pl.ds(c, own, stride=cuts), :] = residual[:, at]
        wide_rows[pl.ds(c, own, stride=cuts), :] = residual[:, at] * scale_rows * post_gain[:, at]
    tiles[...] = wide_rows[0 : own * cuts, :].astype(jnp.bfloat16).reshape(tiles.shape)
    for one in tables:
        one.wait()

    def fill(target, ref, at):
        for c in range(cap):
            ref[at * cap + c] = tiles[jnp.clip(idx_s[c, target], 0, own - 1)]

    def part(ref, t):
        return ref.at[pl.ds(t * cap, cap)]

    def dispatch(t):
        return pltpu.make_async_remote_copy(
            src_ref=part(outgoing, t),
            dst_ref=part(arrived, me),
            send_sem=send_out.at[t],
            recv_sem=recv_out.at[me],
            device_id=neighbour(i, h, t),
            device_id_type=MESH,
        )

    def between(source):
        return pltpu.make_async_remote_copy(
            src_ref=part(arrived, source),
            dst_ref=part(arrived, source),
            send_sem=send_back.at[source],
            recv_sem=recv_out.at[source],
            device_id=(source // 4, lax.rem(source, 4)),
            device_id_type=MESH,
        )

    def give_back(source):
        return pltpu.make_async_remote_copy(
            src_ref=part(arrived, source),
            dst_ref=part(returned, me),
            send_sem=send_back.at[source],
            recv_sem=recv_back.at[me],
            device_id=(source // 4, lax.rem(source, 4)),
            device_id_type=MESH,
        )

    def come_back(expert):
        return pltpu.make_async_remote_copy(
            src_ref=part(arrived, expert),
            dst_ref=part(returned, expert),
            send_sem=send_back.at[expert],
            recv_sem=recv_back.at[expert],
            device_id=(expert // 4, lax.rem(expert, 4)),
            device_id_type=MESH,
        )

    def post(t, c):
        ts, th = neighbour(i, h, t)
        fill(ts * 4 + th, outgoing, t)
        dispatch(t).start()
        return c

    lax.fori_loop(1, devices, post, 0)
    fill(me, arrived, me)
    first_loads[5].wait()
    load(gate_hbm, gate, 3).wait()
    load(down_hbm, down, 4).wait()
    size = batch.shape[0]
    each = size // cap

    def work(k, c):
        def await_one(t, c):
            source = k * each + t
            when(source != me, lambda: between(source).wait_recv())
            return c

        lax.fori_loop(0, each, await_one, 0)
        place = pl.ds(k * size, size)
        wide_rows[...] = arrived[place].astype(jnp.float32).reshape(wide_rows.shape)
        for c in range(cuts):
            batch[:, c * 128 : (c + 1) * 128] = wide_rows[pl.ds(c, size, stride=cuts), :].astype(
                jnp.bfloat16
            )
        gate_proj = jnp.dot(batch[...], gate[...], preferred_element_type=jnp.float32)
        up_proj = jnp.dot(batch[...], up[...], preferred_element_type=jnp.float32)
        hidden = (gate_proj / (1.0 + jnp.exp(-gate_proj)) * up_proj).astype(jnp.bfloat16)
        result = jnp.dot(hidden, down[...], preferred_element_type=jnp.float32)
        for c in range(cuts):
            wide_rows[pl.ds(c, size, stride=cuts), :] = result[:, c * 128 : (c + 1) * 128]
        arrived[place] = wide_rows[...].astype(jnp.bfloat16).reshape(size, cuts, 128)

        def answer(t, c):
            source = k * each + lax.rem(t * 13 + me, each)
            when(source != me, lambda: give_back(source).start())
            return c

        lax.fori_loop(0, each, answer, 0)
        return c

    lax.fori_loop(0, devices // each, work, 0)
    returned[pl.ds(me * cap, cap)] = arrived[pl.ds(me * cap, cap)]

    def settle(expert, c):
        when(expert != me, lambda: come_back(expert).wait_recv())
        return c

    lax.fori_loop(0, devices, settle, 0)

    def combine(t, c):
        place = pl.ds(pl.multiple_of(t * cuts, cuts), cuts)
        total = jnp.zeros((cuts, 128), jnp.float32)
        for n in range(ids_ref.shape[1]):
            total = total + returned[jnp.clip(slot_s[t, n], 0, devices * cap - 1)].astype(jnp.float32) * mix_s[t, n]
        home[place, :] = home[place, :] + total
        return c

    lax.fori_loop(0, own, combine, 0)
    for c in range(cuts):
        out_ref[:, c * 128 : (c + 1) * 128] = home[pl.ds(c, own, stride=cuts), :].astype(jnp.bfloat16)

    columns(lambda zt: k_column(zt).wait_send())
    peers(lambda pt: when((z < 3) | (pt > p), lambda: v_plane(pt).wait_send()))
    peers(lambda pt: when(pt > p, lambda: k_plane(i, pt).wait_send()))
    columns(lambda zt: v_column(i, zt).wait_send())

    def passed_k(t, c):
        peers(lambda pt: k_plane((z - t) * plane + p, pt).wait_send())
        return c

    lax.fori_loop(1, z + 1, passed_k, 0)
    peers(lambda pt: columns(lambda zt: v_column(z * plane + pt, zt).wait_send()))
    for n in range(chunks):
        to_partner(n).wait_send()
        to_mate(n).wait_send()

    def finish(t, c):
        dispatch(t).wait_send()
        return c

    lax.fori_loop(1, devices, finish, 0)

    def finish_back(source, c):
        when(source != me, lambda: give_back(source).wait_send())
        return c

    lax.fori_loop(0, devices, finish_back, 0)


def layer(small, large, seq_count, cap):
    tokens, wk, wv, wq, wo, gate, up, down = large
    rows, width = tokens.shape
    dim = wk.shape[1]
    heads = wq.shape[1] // dim
    own = rows // 4
    devices = seq_count * 4
    chunks = 4
    wide = width // chunks
    cuts = width // 128
    size = devices * cap // 4
    bf16, f32 = jnp.bfloat16, jnp.float32
    vmem = pl.BlockSpec(memory_space=pltpu.VMEM)
    hbm = pl.BlockSpec(memory_space=pl.ANY)
    dma = pltpu.SemaphoreType.DMA
    return pl.pallas_call(
        functools.partial(layer_kernel, heads, dim, cap),
        out_shape=jax.ShapeDtypeStruct((own, width), bf16),
        in_specs=[vmem] * len(small) + [hbm] * len(large),
        out_specs=vmem,
        scratch_shapes=[
            pltpu.VMEM(tokens.shape, bf16),
            pltpu.VMEM(wk.shape, bf16),
            pltpu.VMEM(wv.shape, bf16),
            pltpu.VMEM(wq.shape, bf16),
            pltpu.VMEM(wo.shape, bf16),
            pltpu.VMEM(up.shape, bf16),
            pltpu.VMEM(tokens.shape, bf16),
            pltpu.VMEM((dim, heads * rows), bf16),
            pltpu.VMEM((seq_count, rows, dim), bf16),
            pltpu.VMEM((seq_count, rows, dim), bf16),
            pltpu.VMEM((1, heads * rows), f32),
            pltpu.VMEM((1, heads * rows), f32),
            pltpu.VMEM((dim, heads * rows), f32),
            pltpu.VMEM((rows, heads * dim), bf16),
            pltpu.VMEM((rows, wide), f32),
            pltpu.VMEM((2 * own, width), f32),
            pltpu.VMEM((chunks, 2 * own, wide), bf16),
            pltpu.VMEM((chunks, 2 * own, wide), bf16),
            pltpu.VMEM((chunks, own, wide), bf16),
            pltpu.VMEM((chunks, own, wide), bf16),
            pltpu.VMEM((own, width), f32),
            pltpu.VMEM((own, devices), jnp.int32),
            pltpu.VMEM((own, devices), f32),
            pltpu.VMEM((8, devices), jnp.int32),
            pltpu.SMEM((own, devices), jnp.int32),
            pltpu.SMEM((own, devices), f32),
            pltpu.SMEM((8, devices), jnp.int32),
            pltpu.VMEM((size * cuts, 128), f32),
            pltpu.VMEM((own * cuts, 128), f32),
            pltpu.VMEM((own, cuts, 128), bf16),
            pltpu.VMEM((devices * cap, cuts, 128), bf16),
            pltpu.VMEM((devices * cap, cuts, 128), bf16),
            pltpu.VMEM((size, width), bf16),
            pltpu.VMEM((devices * cap, cuts, 128), bf16),
            dma((9,)),
            dma((seq_count + 4,)),
            dma((seq_count + 8,)),
            dma((seq_count,)),
            dma((seq_count,)),
            dma((chunks,)),
            dma((chunks,)),
            dma((chunks,)),
            dma((chunks,)),
            dma((devices,)),
            dma((devices,)),
            dma((devices,)),
            dma((devices,)),
        ],
        compiler_params=pltpu.CompilerParams(
            collective_id=0, has_side_effects=True, vmem_limit_bytes=60 << 20
        ),
        name="layer",
    )(*small, *large)


def body(
    tokens,
    input_gain,
    w_query,
    w_key,
    w_value,
    query_gain,
    key_gain,
    w_out,
    post_gain,
    expert_ids,
    route_weights,
    w_gate,
    w_up,
    w_down,
):
    tok_rows = tokens.shape[0]
    head_dim = query_gain.shape[0]
    seq_count = lax.axis_size("seq")
    half_dim = head_dim // 2
    positions = (lax.axis_index("seq") * tok_rows + jnp.arange(tok_rows, dtype=jnp.int32)).astype(jnp.float32)
    frequency = THETA ** (-jnp.arange(half_dim, dtype=jnp.float32) * 2.0 / head_dim)
    angles = positions[:, None] * frequency[None, :]
    cosine, sine = jnp.cos(angles), jnp.sin(angles)
    small = (
        input_gain.reshape(1, -1),
        post_gain.reshape(1, -1),
        query_gain.reshape(1, -1),
        key_gain.reshape(1, -1),
        jnp.concatenate([cosine, cosine], axis=1),
        jnp.concatenate([-sine, sine], axis=1),
        expert_ids,
        route_weights,
    )
    large = (tokens, w_key, w_value, w_query, w_out, w_gate[0], w_up[0], w_down[0])
    return layer(small, large, seq_count, CAPACITY)


def solution(mesh):
    placed = (
        P("seq", None),
        P(),
        P(None, "head"),
        P(None, "head"),
        P(None, "head"),
        P(),
        P(),
        P("head", None),
        P(),
        P(("seq", "head"), None),
        P(("seq", "head"), None),
        P(("seq", "head"), None, None),
        P(("seq", "head"), None, None),
        P(("seq", "head"), None, None),
    )
    return jax.shard_map(
        body, mesh=mesh, in_specs=placed, out_specs=P(("seq", "head"), None), check_vma=False
    )
```

time: 180 us -> 199 us (1.11)
  the two profiles are of different devices: /device:TPU:2 before, /device:TPU:96 now
where the time goes in v3:
time: 199 us
  Pallas kernels  193 us (97%)
  local copies, waits for them, and re-layouts  4.41 us (2%)
    pallas_call x1, Pallas kernels, layer(): pl.pallas_call(functools.partial(layer_kernel, heads, dim, cap), out_shap...  193 us
    unnamed x3, local copies, waits for them, and re-layouts  4.41 us

profile of v3, /device:TPU:96, one launch (start us, length us, event | category | flops | bytes accessed | tf_op | source)
XLA Modules:
  0.0 198.7 jit_solution(7248516639862575622)
XLA Ops:
  0.0 0.5 fusion
  0.6 0.8 pad_maximum_fusion
  1.4 1.4 copy.15.ids_ref
  2.8 1.4 copy.16.score_ref
  4.1 192.9 %layer.1 = bf16[64,2048]{1,0:T(8,128)(2,1)} custom-call(f32[1,2048]{1,0:T(1,128)} %bitcast.10, f32[1,2048]{1,0:T(1,128)} %bitcast.11, f32[1,128]{1,0:T(1,128)} %bitcast.12, f32[1,128]{1,0:T(1,128)} %bitcast.13, f32[256,128]{1,0:T(8,128)} %get-tuple-element.8.cos_ref, f32[256,128]{1,0:T(8,128)} %get-tuple-element.9.sin_ref, s32[64,8]{1,0:T(8,128)} %copy.15.ids_ref, ...), custom_call_target="tpu_custom_call" | custom-call | tf_op jit(solution)/shard_map/layer/pallas_call | solution.py:528
  197.0 1.7 copy.18
  (2 shorter events, 0.0 us)

commit v4 on v3

--- a/solution.py
+++ b/solution.py
@@ -15,12 +15,12 @@
 CAPACITY = 6
 
 
-def neighbour(s, h, step):
+def neighbour(s, h, step, sign):
     z, x, y, core = s // 8, lax.rem(s // 2, 4), lax.rem(s, 2) * 2 + h // 2, lax.rem(h, 2)
     turn = lax.rem(step * 37, 128)
-    z = lax.rem(z + turn // 32, 4)
-    x = lax.rem(x + lax.rem(turn // 8, 4), 4)
-    y = lax.rem(y + lax.rem(turn // 2, 4), 4)
+    z = lax.rem(z + sign * (turn // 32) + 4, 4)
+    x = lax.rem(x + sign * lax.rem(turn // 8, 4) + 4, 4)
+    y = lax.rem(y + sign * lax.rem(turn // 2, 4) + 4, 4)
     core = lax.rem(core + lax.rem(turn, 2), 2)
     return z * 8 + x * 2 + y // 2, lax.rem(y, 2) * 2 + core
 
@@ -93,6 +93,7 @@
     recv_out,
     send_back,
     recv_back,
+    gate_sem,
 ):
     i = lax.axis_index("seq")
     h = lax.axis_index("head")
@@ -215,14 +216,14 @@
             q_t[:, head * rows : (head + 1) * rows] = query.T.astype(jnp.bfloat16)
 
     load(gate_hbm, gate, 3).start()
-    ids = ids_ref[...]
+    ids = ids_ref[...].astype(jnp.float32).T.astype(jnp.int32)
     lane = lax.broadcasted_iota(jnp.int32, (own, devices), 1)
     hits = [ids[:, n : n + 1] == lane for n in range(ids.shape[1])]
     named = sum(jnp.where(hit, 1.0, 0.0) for hit in hits)
     order = [lax.broadcasted_iota(jnp.int32, (own, own), n) for n in range(2)]
     earlier_rows = jnp.where(order[0] > order[1], 1.0, 0.0).astype(jnp.bfloat16)
     rank = jnp.dot(earlier_rows, named.astype(jnp.bfloat16), preferred_element_type=jnp.float32)
-    scores_in = score_ref[...]
+    scores_in = score_ref[...].T
     mixing = scores_in / jnp.sum(scores_in, axis=1, keepdims=True)
     slots = jnp.zeros((own, devices), jnp.int32)
     mixes = jnp.zeros((own, devices), jnp.float32)
@@ -258,7 +259,7 @@
     peers(lambda pt: when(z < 3, lambda: pass_v(pt)))
     scale = dim ** (-0.5) * LOG2E
 
-    def group(g, masked):
+    def arrive(g):
         for u in range(GROUP):
             source = g * GROUP + u
             when((source < i) & (lax.rem(source, plane) != p), lambda: k_plane(source, p).wait_recv())
@@ -266,6 +267,8 @@
                 (source < i) & ((source // plane != z) | (z == 3)),
                 lambda: v_column(source, z).wait_recv(),
             )
+
+    def group(g, masked):
         keys = jnp.concatenate([kbuf[g * GROUP + u] for u in range(GROUP)], axis=0)
         halves = [
             vbuf[g * GROUP + u, dim * w : dim * (w + 1), :]
@@ -293,9 +296,21 @@
             acc[...] = acc[...] * shrink + mixed[:dim]
         m_s[...] = top
 
+    def open_gate():
+        def tell(t, c):
+            other = lax.rem(me + t, devices)
+            pl.semaphore_signal(
+                gate_sem, inc=1, device_id=(other // 4, lax.rem(other, 4)), device_id_type=MESH
+            )
+            return c
+
+        lax.fori_loop(1, devices, tell, 0)
+
+    arrive(last)
     group(last, True)
 
     def earlier(t, c):
+        arrive(last - t)
         group(last - t, False)
         return c
 
@@ -381,30 +396,20 @@
     def dispatch(t):
         return pltpu.make_async_remote_copy(
             src_ref=part(outgoing, t),
-            dst_ref=part(arrived, me),
+            dst_ref=part(arrived, t),
             send_sem=send_out.at[t],
-            recv_sem=recv_out.at[me],
-            device_id=neighbour(i, h, t),
+            recv_sem=recv_out.at[t],
+            device_id=neighbour(i, h, t, 1),
             device_id_type=MESH,
         )
 
-    def between(source):
+    def give_back(t):
         return pltpu.make_async_remote_copy(
-            src_ref=part(arrived, source),
-            dst_ref=part(arrived, source),
-            send_sem=send_back.at[source],
-            recv_sem=recv_out.at[source],
-            device_id=(source // 4, lax.rem(source, 4)),
-            device_id_type=MESH,
-        )
-
-    def give_back(source):
-        return pltpu.make_async_remote_copy(
-            src_ref=part(arrived, source),
+            src_ref=part(arrived, t),
             dst_ref=part(returned, me),
-            send_sem=send_back.at[source],
+            send_sem=send_back.at[t],
             recv_sem=recv_back.at[me],
-            device_id=(source // 4, lax.rem(source, 4)),
+            device_id=neighbour(i, h, t, -1),
             device_id_type=MESH,
         )
 
@@ -419,13 +424,15 @@
         )
 
     def post(t, c):
-        ts, th = neighbour(i, h, t)
+        ts, th = neighbour(i, h, t, 1)
         fill(ts * 4 + th, outgoing, t)
         dispatch(t).start()
         return c
 
+    when(z == 3, open_gate)
+    pl.semaphore_wait(gate_sem, jnp.where(z == 3, devices // 4 - 1, devices // 4))
     lax.fori_loop(1, devices, post, 0)
-    fill(me, arrived, me)
+    fill(me, arrived, 0)
     first_loads[5].wait()
     load(gate_hbm, gate, 3).wait()
     load(down_hbm, down, 4).wait()
@@ -434,8 +441,8 @@
 
     def work(k, c):
         def await_one(t, c):
-            source = k * each + t
-            when(source != me, lambda: between(source).wait_recv())
+            step = k * each + t
+            when(step > 0, lambda: dispatch(step).wait_recv())
             return c
 
         lax.fori_loop(0, each, await_one, 0)
@@ -454,15 +461,15 @@
         arrived[place] = wide_rows[...].astype(jnp.bfloat16).reshape(size, cuts, 128)
 
         def answer(t, c):
-            source = k * each + lax.rem(t * 13 + me, each)
-            when(source != me, lambda: give_back(source).start())
+            step = k * each + t
+            when(step > 0, lambda: give_back(step).start())
             return c
 
         lax.fori_loop(0, each, answer, 0)
         return c
 
     lax.fori_loop(0, devices // each, work, 0)
-    returned[pl.ds(me * cap, cap)] = arrived[pl.ds(me * cap, cap)]
+    returned[pl.ds(me * cap, cap)] = arrived[0:cap]
 
     def settle(expert, c):
         when(expert != me, lambda: come_back(expert).wait_recv())
@@ -473,7 +480,7 @@
     def combine(t, c):
         place = pl.ds(pl.multiple_of(t * cuts, cuts), cuts)
         total = jnp.zeros((cuts, 128), jnp.float32)
-        for n in range(ids_ref.shape[1]):
+        for n in range(ids_ref.shape[0]):
             total = total + returned[jnp.clip(slot_s[t, n], 0, devices * cap - 1)].astype(jnp.float32) * mix_s[t, n]
         home[place, :] = home[place, :] + total
         return c
@@ -499,15 +506,10 @@
 
     def finish(t, c):
         dispatch(t).wait_send()
+        give_back(t).wait_send()
         return c
 
     lax.fori_loop(1, devices, finish, 0)
-
-    def finish_back(source, c):
-        when(source != me, lambda: give_back(source).wait_send())
-        return c
-
-    lax.fori_loop(0, devices, finish_back, 0)
 
 
 def layer(small, large, seq_count, cap):
@@ -578,9 +580,10 @@
             dma((devices,)),
             dma((devices,)),
             dma((devices,)),
+            pltpu.SemaphoreType.REGULAR,
         ],
         compiler_params=pltpu.CompilerParams(
-            collective_id=0, has_side_effects=True, vmem_limit_bytes=60 << 20
+            collective_id=0, has_side_effects=True, vmem_limit_bytes=50 << 20
         ),
         name="layer",
     )(*small, *large)
@@ -617,8 +620,8 @@
         key_gain.reshape(1, -1),
         jnp.concatenate([cosine, cosine], axis=1),
         jnp.concatenate([-sine, sine], axis=1),
-        expert_ids,
-        route_weights,
+        expert_ids.T,
+        route_weights.T,
     )
     large = (tokens, w_key, w_value, w_query, w_out, w_gate[0], w_up[0], w_down[0])
     return layer(small, large, seq_count, CAPACITY)

time: 199 us -> 163 us (0.82)
  the two profiles are of different devices: /device:TPU:96 before, /device:TPU:2 now
where the time goes in v4:
time: 163 us; the launch traced here: 161 us
  Pallas kernels  152 us (93%)
  local copies, waits for them, and re-layouts  8.08 us (5%)
    pallas_call x1, Pallas kernels, layer(): pl.pallas_call(functools.partial(layer_kernel, heads, dim, cap), out_shap...  152 us
    unnamed x19, local copies, waits for them, and re-layouts  8.08 us

profile of v4, /device:TPU:2, one launch (start us, length us, event | category | flops | bytes accessed | tf_op | source)
XLA Modules:
  0.0 161.2 jit_solution(13809925511347935167)
XLA Ops:
  0.0 0.5 fusion
  0.6 0.1 pad_maximum_fusion
  0.7 0.0 copy-start
  0.7 1.2 copy-done
  1.9 0.0 copy-start.1
  1.9 1.0 copy-done.1
  3.0 0.0 copy-start.2
  3.0 1.0 copy-done.2
  4.0 0.0 copy-start.3
  4.0 0.7 copy-done.3
  4.7 0.0 copy-start.4
  4.7 0.7 copy-done.4
  5.4 0.0 copy-start.5
  5.4 0.7 copy-done.5
  6.1 0.0 copy-start.6
  6.1 0.7 copy-done.6
  6.8 0.0 copy-start.7
  6.8 0.7 copy-done.7
  7.4 0.0 copy-start.8
  7.4 0.7 copy-done.8
  8.1 152.4 %layer.1 = bf16[64,2048]{1,0:T(8,128)(2,1)S(1)} custom-call(f32[1,2048]{1,0:T(1,128)S(1)} %bitcast.9, f32[1,2048]{1,0:T(1,128)S(1)} %bitcast.10, f32[1,128]{1,0:T(1,128)S(1)} %bitcast.13, f32[1,128]{1,0:T(1,128)S(1)} %bitcast.14, f32[256,128]{1,0:T(8,128)S(1)} %get-tuple-element.8.cos_ref, f32[256,128]{1,0:T(8,128)S(1)} %get-tuple-element.9.sin_ref, ...), custom_call_target="tpu_custom_call" | custom-call | tf_op jit(solution)/shard_map/layer/pallas_call | solution.py:530
  160.5 0.7 copy.16
  (2 shorter events, 0.0 us)
Async XLA Ops:
  0.7 1.2 copy-start
  1.9 1.0 copy-start.1
  3.0 1.0 copy-start.2
  4.0 0.7 copy-start.3
  4.7 0.7 copy-start.4
  5.4 0.7 copy-start.5
  6.1 0.7 copy-start.6
  6.8 0.7 copy-start.7
  7.4 0.7 copy-start.8

commit v5 on v4

--- a/solution.py
+++ b/solution.py
@@ -251,12 +251,15 @@
 
     lax.fori_loop(1, z + 1, pass_k, 0)
 
-    def pass_v(pt):
-        source = z * plane + pt
-        v_column(source, z).wait_recv()
-        columns(lambda zt: v_column(source, zt).start())
-
-    peers(lambda pt: when(z < 3, lambda: pass_v(pt)))
+    def pass_v(zt):
+        def one(pt):
+            source = z * plane + pt
+            when(zt == z + 1, lambda: v_column(source, z).wait_recv())
+            v_column(source, zt).start()
+
+        peers(one)
+
+    columns(pass_v)
     scale = dim ** (-0.5) * LOG2E
 
     def arrive(g):
@@ -525,7 +528,7 @@
     size = devices * cap // 4
     bf16, f32 = jnp.bfloat16, jnp.float32
     vmem = pl.BlockSpec(memory_space=pltpu.VMEM)
-    hbm = pl.BlockSpec(memory_space=pl.ANY)
+    hbm = pl.BlockSpec(memory_space=pltpu.HBM)
     dma = pltpu.SemaphoreType.DMA
     return pl.pallas_call(
         functools.partial(layer_kernel, heads, dim, cap),
@@ -583,7 +586,7 @@
             pltpu.SemaphoreType.REGULAR,
         ],
         compiler_params=pltpu.CompilerParams(
-            collective_id=0, has_side_effects=True, vmem_limit_bytes=50 << 20
+            collective_id=0, has_side_effects=True, vmem_limit_bytes=60 << 20
         ),
         name="layer",
     )(*small, *large)

time: 163 us -> 158 us (0.969)
  local copies, waits for them, and re-layouts: 8.08 us -> 1.67 us
  Pallas kernels: 152 us -> 154 us
    unnamed x19 -> x1, local copies, waits for them, and re-layouts: 8.08 us -> 1.67 us
where the time goes in v5:
time: 158 us; the launch traced here: 157 us
  Pallas kernels  154 us (97%)
  local copies, waits for them, and re-layouts  1.67 us (1%)
    pallas_call x1, Pallas kernels, layer(): pl.pallas_call(functools.partial(layer_kernel, heads, dim, cap), out_shap...  154 us

profile of v5, /device:TPU:2, one launch (start us, length us, event | category | flops | bytes accessed | tf_op | source)
XLA Modules:
  0.0 157.0 jit_solution(12386306595930964335)
XLA Ops:
  0.0 0.5 fusion
  0.6 0.8 pad_maximum_fusion
  1.4 153.9 %layer.1 = bf16[64,2048]{1,0:T(8,128)(2,1)} custom-call(f32[1,2048]{1,0:T(1,128)} %bitcast.12, f32[1,2048]{1,0:T(1,128)} %bitcast.13, f32[1,128]{1,0:T(1,128)} %bitcast.16, f32[1,128]{1,0:T(1,128)} %bitcast.17, f32[256,128]{1,0:T(8,128)} %get-tuple-element.8.cos_ref, f32[256,128]{1,0:T(8,128)} %get-tuple-element.9.sin_ref, s32[8,64]{1,0:T(8,128)} %bitcast.14, ...), custom_call_target="tpu_custom_call" | custom-call | tf_op jit(solution)/shard_map/layer/pallas_call | solution.py:533
  155.3 1.7 %copy.16 = bf16[64,2048]{1,0:T(8,128)(2,1)} copy(bf16[64,2048]{1,0:T(8,128)(2,1)} %layer.1) | data formatting | bytes 524288
  (2 shorter events, 0.0 us)

commit v6 on v5

--- a/solution.py
+++ b/solution.py
@@ -29,14 +29,14 @@
     heads,
     dim,
     cap,
-    in_gain,
-    post_gain,
-    q_gain,
-    k_gain,
     cos_ref,
     sin_ref,
-    ids_ref,
-    score_ref,
+    in_gain_hbm,
+    post_gain_hbm,
+    q_gain_hbm,
+    k_gain_hbm,
+    ids_hbm,
+    score_hbm,
     tok_hbm,
     wk_hbm,
     wv_hbm,
@@ -46,6 +46,12 @@
     up_hbm,
     down_hbm,
     out_ref,
+    in_gain,
+    post_gain,
+    q_gain,
+    k_gain,
+    ids_ref,
+    score_ref,
     tok_ref,
     wk_ref,
     wv_ref,
@@ -122,7 +128,15 @@
         load(wo_hbm, wo, 4),
         load(up_hbm, up, 5),
     ]
-    for one in first_loads:
+    small_loads = [
+        load(in_gain_hbm, in_gain, 9),
+        load(post_gain_hbm, post_gain, 10),
+        load(q_gain_hbm, q_gain, 11),
+        load(k_gain_hbm, k_gain, 12),
+        load(ids_hbm, ids_ref, 13),
+        load(score_hbm, score_ref, 14),
+    ]
+    for one in first_loads[0:3] + small_loads + first_loads[3:]:
         one.start()
     for u in range(GROUP):
 
@@ -148,6 +162,8 @@
         return vectors * cos_ref[...] + pltpu.roll(vectors, dim // 2, 1) * sin_ref[...]
 
     first_loads[0].wait()
+    for one in small_loads:
+        one.wait()
     tokens = tok_ref[...].astype(jnp.float32)
     mean_sq = jnp.mean(tokens * tokens, axis=-1, keepdims=True)
     normed[...] = (tokens * lax.rsqrt(mean_sq + EPSILON) * in_gain[...]).astype(jnp.bfloat16)
@@ -216,6 +232,23 @@
             q_t[:, head * rows : (head + 1) * rows] = query.T.astype(jnp.bfloat16)
 
     load(gate_hbm, gate, 3).start()
+    def pass_k(t, c):
+        source = (z - t) * plane + p
+        k_plane(source, p).wait_recv()
+        peers(lambda pt: k_plane(source, pt).start())
+        return c
+
+    lax.fori_loop(1, z + 1, pass_k, 0)
+
+    def pass_v(zt):
+        def one(pt):
+            source = z * plane + pt
+            when(zt == z + 1, lambda: v_column(source, z).wait_recv())
+            v_column(source, zt).start()
+
+        peers(one)
+
+    columns(pass_v)
     ids = ids_ref[...].astype(jnp.float32).T.astype(jnp.int32)
     lane = lax.broadcasted_iota(jnp.int32, (own, devices), 1)
     hits = [ids[:, n : n + 1] == lane for n in range(ids.shape[1])]
@@ -242,24 +275,6 @@
     tables = [load(slot_v, slot_s, 6), load(mix_v, mix_s, 7), load(idx_v, idx_s, 8)]
     for one in tables:
         one.start()
-
-    def pass_k(t, c):
-        source = (z - t) * plane + p
-        k_plane(source, p).wait_recv()
-        peers(lambda pt: k_plane(source, pt).start())
-        return c
-
-    lax.fori_loop(1, z + 1, pass_k, 0)
-
-    def pass_v(zt):
-        def one(pt):
-            source = z * plane + pt
-            when(zt == z + 1, lambda: v_column(source, z).wait_recv())
-            v_column(source, zt).start()
-
-        peers(one)
-
-    columns(pass_v)
     scale = dim ** (-0.5) * LOG2E
 
     def arrive(g):
@@ -474,45 +489,49 @@
     lax.fori_loop(0, devices // each, work, 0)
     returned[pl.ds(me * cap, cap)] = arrived[0:cap]
 
+    columns(lambda zt: k_column(zt).wait_send())
+    peers(lambda pt: when((z < 3) | (pt > p), lambda: v_plane(pt).wait_send()))
+    peers(lambda pt: when(pt > p, lambda: k_plane(i, pt).wait_send()))
+    columns(lambda zt: v_column(i, zt).wait_send())
+
+    def passed_k(t, c):
+        peers(lambda pt: k_plane((z - t) * plane + p, pt).wait_send())
+        return c
+
+    lax.fori_loop(1, z + 1, passed_k, 0)
+    peers(lambda pt: columns(lambda zt: v_column(z * plane + pt, zt).wait_send()))
+    for n in range(chunks):
+        to_partner(n).wait_send()
+        to_mate(n).wait_send()
+
+    def finish(t, c):
+        dispatch(t).wait_send()
+        give_back(t).wait_send()
+        return c
+
+    lax.fori_loop(1, devices, finish, 0)
+
     def settle(expert, c):
         when(expert != me, lambda: come_back(expert).wait_recv())
         return c
 
     lax.fori_loop(0, devices, settle, 0)
 
-    def combine(t, c):
+    def combine_one(t):
         place = pl.ds(pl.multiple_of(t * cuts, cuts), cuts)
         total = jnp.zeros((cuts, 128), jnp.float32)
         for n in range(ids_ref.shape[0]):
             total = total + returned[jnp.clip(slot_s[t, n], 0, devices * cap - 1)].astype(jnp.float32) * mix_s[t, n]
         home[place, :] = home[place, :] + total
-        return c
-
-    lax.fori_loop(0, own, combine, 0)
+
+    def combine(t, c):
+        for n in range(4):
+            combine_one(t * 4 + n)
+        return c
+
+    lax.fori_loop(0, own // 4, combine, 0)
     for c in range(cuts):
         out_ref[:, c * 128 : (c + 1) * 128] = home[pl.ds(c, own, stride=cuts), :].astype(jnp.bfloat16)
-
-    columns(lambda zt: k_column(zt).wait_send())
-    peers(lambda pt: when((z < 3) | (pt > p), lambda: v_plane(pt).wait_send()))
-    peers(lambda pt: when(pt > p, lambda: k_plane(i, pt).wait_send()))
-    columns(lambda zt: v_column(i, zt).wait_send())
-
-    def passed_k(t, c):
-        peers(lambda pt: k_plane((z - t) * plane + p, pt).wait_send())
-        return c
-
-    lax.fori_loop(1, z + 1, passed_k, 0)
-    peers(lambda pt: columns(lambda zt: v_column(z * plane + pt, zt).wait_send()))
-    for n in range(chunks):
-        to_partner(n).wait_send()
-        to_mate(n).wait_send()
-
-    def finish(t, c):
-        dispatch(t).wait_send()
-        give_back(t).wait_send()
-        return c
-
-    lax.fori_loop(1, devices, finish, 0)
 
 
 def layer(small, large, seq_count, cap):
@@ -533,9 +552,10 @@
     return pl.pallas_call(
         functools.partial(layer_kernel, heads, dim, cap),
         out_shape=jax.ShapeDtypeStruct((own, width), bf16),
-        in_specs=[vmem] * len(small) + [hbm] * len(large),
+        in_specs=[vmem] * 2 + [hbm] * (len(small) - 2 + len(large)),
         out_specs=vmem,
         scratch_shapes=[
+            *(pltpu.VMEM(a.shape, a.dtype) for a in small[2:]),
             pltpu.VMEM(tokens.shape, bf16),
             pltpu.VMEM(wk.shape, bf16),
             pltpu.VMEM(wv.shape, bf16),
@@ -570,7 +590,7 @@
             pltpu.VMEM((devices * cap, cuts, 128), bf16),
             pltpu.VMEM((size, width), bf16),
             pltpu.VMEM((devices * cap, cuts, 128), bf16),
-            dma((9,)),
+            dma((15,)),
             dma((seq_count + 4,)),
             dma((seq_count + 8,)),
             dma((seq_count,)),
@@ -617,12 +637,12 @@
     angles = positions[:, None] * frequency[None, :]
     cosine, sine = jnp.cos(angles), jnp.sin(angles)
     small = (
+        jnp.concatenate([cosine, cosine], axis=1),
+        jnp.concatenate([-sine, sine], axis=1),
         input_gain.reshape(1, -1),
         post_gain.reshape(1, -1),
         query_gain.reshape(1, -1),
         key_gain.reshape(1, -1),
-        jnp.concatenate([cosine, cosine], axis=1),
-        jnp.concatenate([-sine, sine], axis=1),
         expert_ids.T,
         route_weights.T,
     )

time: 158 us -> 157 us (level)
  Pallas kernels: 154 us -> 152 us
where the time goes in v6:
time: 157 us; the launch traced here: 156 us
  Pallas kernels  152 us (97%)
  local copies, waits for them, and re-layouts  1.67 us (1%)
    pallas_call x1, Pallas kernels, layer(): pl.pallas_call(functools.partial(layer_kernel, heads, dim, cap), out_shap...  152 us

profile of v6, /device:TPU:2, one launch (start us, length us, event | category | flops | bytes accessed | tf_op | source)
XLA Modules:
  0.0 155.5 jit_solution(16650449162707287281)
XLA Ops:
  0.0 0.5 fusion
  0.6 0.8 pad_maximum_fusion
  1.4 152.5 %layer.1 = bf16[64,2048]{1,0:T(8,128)(2,1)} custom-call(f32[256,128]{1,0:T(8,128)} %get-tuple-element.8.cos_ref, f32[256,128]{1,0:T(8,128)} %get-tuple-element.9.sin_ref, f32[1,2048]{1,0:T(1,128)} %bitcast.12, f32[1,2048]{1,0:T(1,128)} %bitcast.13, f32[1,128]{1,0:T(1,128)} %bitcast.16, f32[1,128]{1,0:T(1,128)} %bitcast.17, s32[8,64]{1,0:T(8,128)} %bitcast.14, ...), custom_call_target="tpu_custom_call" | custom-call | tf_op jit(solution)/shard_map/layer/pallas_call | solution.py:552
  153.9 1.7 %copy.16 = bf16[64,2048]{1,0:T(8,128)(2,1)} copy(bf16[64,2048]{1,0:T(8,128)(2,1)} %layer.1) | data formatting | bytes 524288
  (2 shorter events, 0.0 us)

commit v7 on v6

--- a/solution.py
+++ b/solution.py
@@ -541,7 +541,7 @@
     heads = wq.shape[1] // dim
     own = rows // 4
     devices = seq_count * 4
-    chunks = 4
+    chunks = 8
     wide = width // chunks
     cuts = width // 128
     size = devices * cap // 4
@@ -633,12 +633,12 @@
     seq_count = lax.axis_size("seq")
     half_dim = head_dim // 2
     positions = (lax.axis_index("seq") * tok_rows + jnp.arange(tok_rows, dtype=jnp.int32)).astype(jnp.float32)
-    frequency = THETA ** (-jnp.arange(half_dim, dtype=jnp.float32) * 2.0 / head_dim)
+    frequency = THETA ** (-(jnp.arange(head_dim) % half_dim).astype(jnp.float32) * 2.0 / head_dim)
     angles = positions[:, None] * frequency[None, :]
-    cosine, sine = jnp.cos(angles), jnp.sin(angles)
+    sign = jnp.where(jnp.arange(head_dim) < half_dim, -1.0, 1.0).astype(jnp.float32)
     small = (
-        jnp.concatenate([cosine, cosine], axis=1),
-        jnp.concatenate([-sine, sine], axis=1),
+        jnp.cos(angles),
+        jnp.sin(angles) * sign,
         input_gain.reshape(1, -1),
         post_gain.reshape(1, -1),
         query_gain.reshape(1, -1),

time: 157 us -> 157 us (level)
  no operation moved by 1% of the time
where the time goes in v7:
time: 157 us; the launch traced here: 156 us
  Pallas kernels  153 us (97%)
  local copies, waits for them, and re-layouts  1.67 us (1%)
    pallas_call x1, Pallas kernels, layer(): pl.pallas_call(functools.partial(layer_kernel, heads, dim, cap), out_shap...  153 us

profile of v7, /device:TPU:2, one launch (start us, length us, event | category | flops | bytes accessed | tf_op | source)
XLA Modules:
  0.0 155.5 jit_solution(8900987305525837220)
XLA Ops:
  0.0 1.2 fusion
  1.3 152.6 %layer.1 = bf16[64,2048]{1,0:T(8,128)(2,1)} custom-call(f32[256,128]{1,0:T(8,128)} %get-tuple-element.6.cos_ref, f32[256,128]{1,0:T(8,128)} %get-tuple-element.5.sin_ref, f32[1,2048]{1,0:T(1,128)} %bitcast.12, f32[1,2048]{1,0:T(1,128)} %bitcast.13, f32[1,128]{1,0:T(1,128)} %bitcast.16, f32[1,128]{1,0:T(1,128)} %bitcast.17, s32[8,64]{1,0:T(8,128)} %bitcast.14, ...), custom_call_target="tpu_custom_call" | custom-call | tf_op jit(solution)/shard_map/layer/pallas_call | solution.py:552
  153.8 1.7 %copy.16 = bf16[64,2048]{1,0:T(8,128)(2,1)} copy(bf16[64,2048]{1,0:T(8,128)(2,1)} %layer.1) | data formatting | bytes 524288
  (2 shorter events, 0.0 us)
